TPU v7x, 256 devices: a whole 4x4x8 slice. The times are simulated.
256 devices in a mesh: gx: 32 (over z, y), gy: 8 (over x, core).
Axes of the slice: x: 4, y: 4, z: 8, core: 2. Of those that a mesh axis runs over, the one named last changes fastest.
Arguments:
- density: float32 [256, 512, 256], P('gx', 'gy'), may hold values from 0.6 to 1.6
- momentum: float32 [3, 256, 512, 256], P(None, 'gx', 'gy'), may hold values from -0.6 to 2.1
- energy: float32 [256, 512, 256], P('gx', 'gy'), may hold values from 2 to 4
- snapshots: bfloat16 [63, 3, 64, 8192], P(None, None, 'gx', 'gy'), may hold values from -3.9 to 9.9
Outputs:
- new_density: float32 [256, 512, 256], P('gx', 'gy')
- new_momentum: float32 [3, 256, 512, 256], P(None, 'gx', 'gy')
- new_energy: float32 [256, 512, 256], P('gx', 'gy')
- pod_factor: float32 [64, 64], replicated
- pod_modes: float32 [64, 3, 64, 8192], P(None, None, 'gx', 'gy')
All inputs are finite; a program needn't handle non-finite values.
Results may differ from a plain program's by a relative error of at most 0.00035.
Values sent between devices are 32-bit elements; how exact they have to be, the bound alone decides.
A program may use at most 128 MiB of HBM per device.

v0:
```python
import jax
import jax.numpy as jnp
from jax import lax
from jax.sharding import PartitionSpec as P

time_step = 0.08
shear_friction_coefficient = 1.5
heat_conduction_coefficient = 1.5


def padded_2(block, sides, width):
    for axis, dim in sides:
        count = lax.axis_size(axis)
        forward = [(i, i + 1) for i in range(count - 1)]
        forward.append((count - 1, 0))
        backward = [(target, source) for source, target in forward]
        low = lax.ppermute(
            lax.slice_in_dim(block, block.shape[dim] - width, None, axis=dim), axis, forward
        )
        high = lax.ppermute(lax.slice_in_dim(block, 0, width, axis=dim), axis, backward)
        block = jnp.concatenate([low, block, high], axis=dim)
    return block


def from_partner(value, axis, apart):
    mask = 2**apart
    pairs = [(source, source ^ mask) for source in range(lax.axis_size(axis))]
    return lax.ppermute(value, axis, pairs)


def sheet_curvature_operator(field):
    return (
        field[..., 2:, 1:-1, :]
        + field[..., :-2, 1:-1, :]
        + field[..., 1:-1, 2:, :]
        + field[..., 1:-1, :-2, :]
        - 4.0 * field[..., 1:-1, 1:-1, :]
    )


def boundary_couple(center, copied):
    if copied:
        upper_cell = jnp.concatenate([center[..., 1:], center[..., -1:]], axis=-1)
        lower_cell = jnp.concatenate([center[..., :1], center[..., :-1]], axis=-1)
    else:
        zeros_row = jnp.zeros_like(center[..., :1])
        upper_cell = jnp.concatenate([center[..., 1:], zeros_row], axis=-1)
        lower_cell = jnp.concatenate([zeros_row, center[..., :-1]], axis=-1)
    return (upper_cell, lower_cell)


def tendency(padded):
    mass_density_grid = padded[0]
    momenta = padded[1:4]
    total_energy_grid = padded[4]
    velocity = momenta / mass_density_grid
    heat_condition_fields = total_energy_grid / mass_density_grid
    vel_center = velocity[:, 1:-1, 1:-1, :]
    vel_upper, vel_lower = boundary_couple(vel_center, False)
    velocity_second_derivative_sum = (
        sheet_curvature_operator(velocity) + vel_upper + vel_lower - 2.0 * vel_center
    )
    central_heat_value = heat_condition_fields[1:-1, 1:-1, :]
    upper_neighbour_heat, lower_neighbour_heat = boundary_couple(central_heat_value, True)
    heat_curvature_sum = (
        sheet_curvature_operator(heat_condition_fields)
        + upper_neighbour_heat
        + lower_neighbour_heat
        - 2.0 * central_heat_value
    )
    normal_upper, normal_lower = boundary_couple(momenta[2][1:-1, 1:-1, :], False)
    flux_spread_rate = 0.5 * (
        momenta[0][2:, 1:-1, :]
        - momenta[0][:-2, 1:-1, :]
        + (momenta[1][1:-1, 2:, :] - momenta[1][1:-1, :-2, :])
        + (normal_upper - normal_lower)
    )
    return jnp.concatenate(
        [
            (-flux_spread_rate)[None],
            shear_friction_coefficient * velocity_second_derivative_sum,
            (heat_conduction_coefficient * heat_curvature_sum)[None],
        ],
        axis=0,
    )


def widen(state):
    return padded_2(state, (("gx", 1), ("gy", 2)), 1)


def matvec_rows(selector, matrix):
    return jnp.dot(
        selector, matrix, precision=lax.Precision.HIGHEST, preferred_element_type=jnp.float32
    )


def cholesky_upper(gram):
    order = gram.shape[0]
    position = jnp.arange(order)

    def column_step(index, carry):
        working, factor = carry
        selector = (position == index).astype(jnp.float32)
        chosen_row = matvec_rows(selector, working)
        pivot = jnp.sum(chosen_row * selector)
        scaled_row = jnp.where(position >= index, chosen_row / jnp.sqrt(pivot), 0.0)
        factor = factor + selector[:, None] * scaled_row[None, :]
        working = working - scaled_row[:, None] * scaled_row[None, :]
        return (working, factor)

    start = (gram, jnp.zeros_like(gram))
    working, factor = lax.fori_loop(0, order, column_step, start)
    return factor


def invert_upper(factor):
    order = factor.shape[0]
    position = jnp.arange(order)

    def back_step(count, inverse):
        index = order - 1 - count
        selector = (position == index).astype(jnp.float32)
        factor_row = matvec_rows(selector, factor)
        pivot = jnp.sum(factor_row * selector)
        strict_row = jnp.where(position > index, factor_row, 0.0)
        new_row = (selector - matvec_rows(strict_row, inverse)) / pivot
        return inverse + selector[:, None] * new_row[None, :]

    return lax.fori_loop(0, order, back_step, jnp.zeros_like(factor))


def inner_gram(own_factor):
    return jnp.dot(
        own_factor.T,
        own_factor,
        precision=lax.Precision.HIGHEST,
        preferred_element_type=jnp.float32,
    )


def combine(own_factor, peer_factor):
    return cholesky_upper(inner_gram(own_factor) + inner_gram(peer_factor))


def on_device(density, momentum, energy, snapshots):
    state = jnp.concatenate([density[None], momentum, energy[None]], axis=0)
    sectioned = state + time_step * tendency(widen(state))
    updated = 0.5 * state + 0.5 * (sectioned + time_step * tendency(widen(sectioned)))
    coarse_x = updated.shape[1] // 4
    coarse_y = updated.shape[2] // 4
    coarse_z = updated.shape[3] // 4
    velocity = updated[1:4] / updated[0]
    coarse = velocity.reshape(3, coarse_x, 4, coarse_y, 4, coarse_z, 4).mean(axis=(2, 4, 6))
    coarse = coarse.reshape(1, -1)
    stored = snapshots.reshape(snapshots.shape[0], -1)
    stored_gram = jnp.dot(stored, stored.T, preferred_element_type=jnp.float32)
    cross_row = jnp.dot(
        coarse, stored.T, precision=lax.Precision.HIGHEST, preferred_element_type=jnp.float32
    )
    coarse_self = jnp.dot(
        coarse, coarse.T, precision=lax.Precision.HIGHEST, preferred_element_type=jnp.float32
    )
    upper_rows = jnp.concatenate([stored_gram, cross_row.T], axis=1)
    lower_row = jnp.concatenate([cross_row, coarse_self], axis=1)
    local_gram = jnp.concatenate([upper_rows, lower_row], axis=0)
    rows_all = stored.shape[1] * lax.axis_size("gx") * lax.axis_size("gy")
    factor = cholesky_upper(local_gram / rows_all)
    for rung_bit in range(lax.axis_size("gx").bit_length() - 1):
        factor = combine(factor, from_partner(factor, "gx", rung_bit))
    for rung_bit in range(lax.axis_size("gy").bit_length() - 1):
        factor = combine(factor, from_partner(factor, "gy", rung_bit))
    local_columns = jnp.concatenate([stored.astype(jnp.float32), coarse], axis=0)
    inverse = invert_upper(factor)
    modes = jnp.dot(
        inverse.T,
        local_columns,
        precision=lax.Precision.HIGHEST,
        preferred_element_type=jnp.float32,
    )
    pod_modes = modes.reshape(snapshots.shape[0] + 1, 3, snapshots.shape[2], snapshots.shape[3])
    return (updated[0], updated[1:4], updated[4], factor, pod_modes)


def solution(mesh):
    placed = (
        P("gx", "gy", None),
        P(None, "gx", "gy", None),
        P("gx", "gy", None),
        P(None, None, "gx", "gy"),
    )
    return jax.shard_map(
        on_device,
        mesh=mesh,
        in_specs=placed,
        out_specs=(
            P("gx", "gy", None),
            P(None, "gx", "gy", None),
            P("gx", "gy", None),
            P(),
            P(None, None, "gx", "gy"),
        ),
        check_vma=False,
    )
```

profile of v0, /device:TPU:1, one launch (start us, length us, event | category | flops | bytes accessed | tf_op | source)
XLA Modules:
  0.0 1185.4 jit_solution(10393516203676375234)
XLA Ops:
  0.7 2.1 pad_maximum_fusion.2
  2.8 2.2 collective-permute-start
  5.0 6.8 collective-permute-start.1
  11.9 7.3 collective-permute-done
  19.3 2.3 collective-permute-start.2
  21.6 1.2 collective-permute-done.2
  22.8 2.3 collective-permute-done.3
  27.6 0.9 fusion.93
  30.3 5.1 collective-permute-start.5
  35.4 7.5 collective-permute-done.4
  42.9 0.8 pad_maximum_fusion.5
  44.6 1.0 convolution_bitcast_fusion.11
  45.6 3.2 reshape.132
  48.9 2.4 convert_element_type.115
  51.4 2.2 pad_maximum_fusion.1
  55.3 0.9 fusion.88
  58.8 0.9 slice_bitcast_fusion.10
  59.7 1.4 broadcast_divide_fusion
  61.1 53.3 %reshape.131 = f32[3,2,4,16,4,64,4]{6,5,4,3,2,1,0:T(8,128)} reshape(f32[3,8,64,256]{3,2,1,0:T(8,128)S(1)} %get-tuple-element.1164) | data formatting | bytes 3145728 | tf_op jit(solution)/shard_map/reshape | solution.py:154
  114.5 17.9 %reduce_sum.139 = f32[3,2,16,64]{3,2,1,0:T(8,128)S(1)} reduce(f32[3,2,4,16,4,64,4]{6,5,4,3,2,1,0:T(8,128)} %reshape.131, f32[]{:T(128)} %constant.214.clone.1), dimensions={2,4,6}, to_apply=%region_0.0 | reduce | flops 387072 | bytes 1597444 | tf_op jit(solution)/shard_map/reduce_sum | solution.py:154
  134.8 100.3 %while.168 = (s32[]{:T(128)}, f32[64,64]{1,0:T(8,128)S(1)}, f32[64,64]{1,0:T(8,128)S(1)}, s32[]{:T(128)}, s32[]{:T(128)}) while((s32[]{:T(128)}, f32[64,64]{1,0:T(8,128)S(1)}, f32[64,64]{1,0:T(8,128)S(1)}, s32[]{:T(128)}, s32[]{:T(128)}) %tuple.391), condition=%wide.region_3.4_spmd.clone.clone, body=%wide.region_1.3_spmd.clone.clone.sunk | while | flops 70210 | bytes 83555 | solution.py:113
  235.6 2.4 collective-permute-done.8
  238.2 100.3 %while.169 = (s32[]{:T(128)}, f32[64,64]{1,0:T(8,128)S(1)}, f32[64,64]{1,0:T(8,128)S(1)}, s32[]{:T(128)}, s32[]{:T(128)}) while((s32[]{:T(128)}, f32[64,64]{1,0:T(8,128)S(1)}, f32[64,64]{1,0:T(8,128)S(1)}, s32[]{:T(128)}, s32[]{:T(128)}) %tuple.394), condition=%wide.region_6.7_spmd.clone.clone, body=%wide.region_4.6_spmd.clone.clone.sunk | while | flops 70210 | bytes 83555 | solution.py:113
  338.9 4.0 collective-permute-done.9
  343.2 100.3 %while.170 = (s32[]{:T(128)}, f32[64,64]{1,0:T(8,128)S(1)}, f32[64,64]{1,0:T(8,128)S(1)}, s32[]{:T(128)}, s32[]{:T(128)}) while((s32[]{:T(128)}, f32[64,64]{1,0:T(8,128)S(1)}, f32[64,64]{1,0:T(8,128)S(1)}, s32[]{:T(128)}, s32[]{:T(128)}) %tuple.397), condition=%wide.region_9.10_spmd.clone.clone, body=%wide.region_7.9_spmd.clone.clone.sunk | while | flops 70210 | bytes 83555 | solution.py:113
  443.9 2.5 collective-permute-done.10
  446.6 100.3 %while.171 = (s32[]{:T(128)}, f32[64,64]{1,0:T(8,128)S(1)}, f32[64,64]{1,0:T(8,128)S(1)}, s32[]{:T(128)}, s32[]{:T(128)}) while((s32[]{:T(128)}, f32[64,64]{1,0:T(8,128)S(1)}, f32[64,64]{1,0:T(8,128)S(1)}, s32[]{:T(128)}, s32[]{:T(128)}) %tuple.400), condition=%wide.region_12.13_spmd.clone.clone, body=%wide.region_10.12_spmd.clone.clone.sunk | while | flops 70210 | bytes 83555 | solution.py:113
  547.0 2.3 collective-permute-start.11
  549.6 1.4 collective-permute-done.11
  551.2 100.3 %while.172 = (s32[]{:T(128)}, f32[64,64]{1,0:T(8,128)S(1)}, f32[64,64]{1,0:T(8,128)S(1)}, s32[]{:T(128)}, s32[]{:T(128)}) while((s32[]{:T(128)}, f32[64,64]{1,0:T(8,128)S(1)}, f32[64,64]{1,0:T(8,128)S(1)}, s32[]{:T(128)}, s32[]{:T(128)}) %tuple.403), condition=%wide.region_15.16_spmd.clone.clone, body=%wide.region_13.15_spmd.clone.clone.sunk | while | flops 70210 | bytes 83555 | solution.py:113
  651.6 3.7 collective-permute-start.12
  655.6 2.9 collective-permute-done.12
  658.7 100.3 %while.173 = (s32[]{:T(128)}, f32[64,64]{1,0:T(8,128)S(1)}, f32[64,64]{1,0:T(8,128)S(1)}, s32[]{:T(128)}, s32[]{:T(128)}) while((s32[]{:T(128)}, f32[64,64]{1,0:T(8,128)S(1)}, f32[64,64]{1,0:T(8,128)S(1)}, s32[]{:T(128)}, s32[]{:T(128)}) %tuple.406), condition=%wide.region_18.19_spmd.clone.clone, body=%wide.region_16.18_spmd.clone.clone.sunk | while | flops 70210 | bytes 83555 | solution.py:113
  759.0 9.0 collective-permute-start.13
  769.1 100.3 %while.174 = (s32[]{:T(128)}, f32[64,64]{1,0:T(8,128)S(1)}, f32[64,64]{1,0:T(8,128)S(1)}, s32[]{:T(128)}, s32[]{:T(128)}) while((s32[]{:T(128)}, f32[64,64]{1,0:T(8,128)S(1)}, f32[64,64]{1,0:T(8,128)S(1)}, s32[]{:T(128)}, s32[]{:T(128)}) %tuple.409), condition=%wide.region_21.22_spmd.clone.clone, body=%wide.region_19.21_spmd.clone.clone.sunk | while | flops 70210 | bytes 83555 | solution.py:113
  869.8 2.5 collective-permute-done.14
  872.6 100.3 %while.175 = (s32[]{:T(128)}, f32[64,64]{1,0:T(8,128)S(1)}, f32[64,64]{1,0:T(8,128)S(1)}, s32[]{:T(128)}, s32[]{:T(128)}) while((s32[]{:T(128)}, f32[64,64]{1,0:T(8,128)S(1)}, f32[64,64]{1,0:T(8,128)S(1)}, s32[]{:T(128)}, s32[]{:T(128)}) %tuple.412), condition=%wide.region_24.25_spmd.clone.clone, body=%wide.region_22.24_spmd.clone.clone.sunk | while | flops 70210 | bytes 83555 | solution.py:113
  973.7 3.5 collective-permute-done.15
  977.5 100.3 %while.176 = (s32[]{:T(128)}, f32[64,64]{1,0:T(8,128)S(1)}, f32[64,64]{1,0:T(8,128)S(1)}, s32[]{:T(128)}, s32[]{:T(128)}) while((s32[]{:T(128)}, f32[64,64]{1,0:T(8,128)S(1)}, f32[64,64]{1,0:T(8,128)S(1)}, s32[]{:T(128)}, s32[]{:T(128)}) %tuple.415), condition=%wide.region_27.28_spmd.clone.clone, body=%wide.region_25.27_spmd.clone.clone.sunk | while | flops 70210 | bytes 83555 | solution.py:113
  1077.9 103.5 %while.177 = (s32[]{:T(128)}, f32[64,64]{1,0:T(8,128)S(1)}, f32[64,64]{1,0:T(8,128)S(1)}, s32[]{:T(128)}, s32[]{:T(128)}, /*index=5*/s32[]{:T(128)}) while((s32[]{:T(128)}, f32[64,64]{1,0:T(8,128)S(1)}, f32[64,64]{1,0:T(8,128)S(1)}, s32[]{:T(128)}, s32[]{:T(128)}, /*index=5*/s32[]{:T(128)}) %tuple.418), condition=%wide.region_30.31_spmd.clone.clone, body=%wide.region_28.30_spmd.clone.clone.sunk | while | flops 115459 | bytes 67184 | solution.py:130
  1078.6 0.8 fusion.252
  1080.3 0.8 fusion.252
  1081.9 0.8 fusion.252
  1083.5 0.8 fusion.252
  1085.1 0.8 fusion.252
  1093.2 0.8 fusion.252
  1181.4 1.5 fusion.94
  1182.9 2.5 reshape.133
  (2665 shorter events, 594.9 us)
Async XLA Ops:
  0.6 18.6 %copy-start = (f32[3,8,64,256]{3,2,1,0:T(8,128)S(1)}, f32[3,8,64,256]{3,2,1,0:T(8,128)}, u32[]{:S(2)}) copy-start(f32[3,8,64,256]{3,2,1,0:T(8,128)} %param.25) | copy-start | bytes 4718596
  0.6 18.6 %copy-start.2 = (f32[8,64,256]{2,1,0:T(8,128)S(1)}, f32[8,64,256]{2,1,0:T(8,128)}, u32[]{:S(2)}) copy-start(f32[8,64,256]{2,1,0:T(8,128)} %param.26) | copy-start | bytes 1572868
  0.7 18.6 %copy-start.4 = (f32[8,64,256]{2,1,0:T(8,128)S(1)}, f32[8,64,256]{2,1,0:T(8,128)}, u32[]{:S(2)}) copy-start(f32[8,64,256]{2,1,0:T(8,128)} %param.24) | copy-start | bytes 1572868
  2.8 16.4 %collective-permute-start = (f32[5,1,64,256]{3,2,1,0:T(8,128)S(1)}, f32[5,1,64,256]{3,2,1,0:T(8,128)S(1)}, u32[]{:S(2)}, u32[]{:S(2)}) collective-permute-start(f32[5,1,64,256]{3,2,1,0:T(8,128)S(1)} %get-tuple-element.1220), channel_id=1, source_target_pairs={{0,8},{8,16},{16,24},{24,32},{32,40},{40,48},{48,56},{56,64},{64,7... | collective-permute-start | bytes 983048 | tf_op jit(solution)/shard_map/ppermute | solution.py:17
  5.0 14.2 %collective-permute-start.1 = (f32[5,1,64,256]{3,2,1,0:T(8,128)S(1)}, f32[5,1,64,256]{3,2,1,0:T(8,128)S(1)}, u32[]{:S(2)}, u32[]{:S(2)}) collective-permute-start(f32[5,1,64,256]{3,2,1,0:T(8,128)S(1)} %get-tuple-element.1221), channel_id=1, source_target_pairs={{8,0},{16,8},{24,16},{32,24},{40,32},{48,40},{56,48},{64,56},{72,6... | collective-permute-start | bytes 983048 | tf_op jit(solution)/shard_map/ppermute | solution.py:20
  19.3 3.5 collective-permute-start.2
  21.6 3.5 collective-permute-start.3
  29.2 0.8 copy-start.7
  29.2 1.0 copy-start.9
  30.1 13.6 %copy-start.1 = (f32[5,8,64,256]{3,2,1,0:T(8,128)}, f32[5,8,64,256]{3,2,1,0:T(8,128)S(1)}, u32[]{:S(2)}) copy-start(f32[5,8,64,256]{3,2,1,0:T(8,128)S(1)} %fusion.80) | copy-start | bytes 7864324
  30.1 14.5 %copy-start.18 = (bf16[63,3,2,1024]{3,2,1,0:T(2,128)(2,1)S(1)}, bf16[63,3,2,1024]{3,2,1,0:T(2,128)(2,1)}, u32[]{:S(2)}) copy-start(bf16[63,3,2,1024]{3,2,1,0:T(2,128)(2,1)} %param.27) | copy-start | bytes 2322436
  30.2 12.7 %collective-permute-start.4 = (f32[5,1,64,256]{3,2,1,0:T(8,128)S(1)}, f32[5,1,64,256]{3,2,1,0:T(8,128)S(1)}, u32[]{:S(2)}, u32[]{:S(2)}) collective-permute-start(f32[5,1,64,256]{3,2,1,0:T(8,128)S(1)} %get-tuple-element.1218), channel_id=1, source_target_pairs={{0,8},{8,16},{16,24},{24,32},{32,40},{40,48},{48,56},{56,64},{64,7... | collective-permute-start | bytes 983048 | tf_op jit(solution)/shard_map/ppermute | solution.py:17
  30.3 12.7 %collective-permute-start.5 = (f32[5,1,64,256]{3,2,1,0:T(8,128)S(1)}, f32[5,1,64,256]{3,2,1,0:T(8,128)S(1)}, u32[]{:S(2)}, u32[]{:S(2)}) collective-permute-start(f32[5,1,64,256]{3,2,1,0:T(8,128)S(1)} %get-tuple-element.1219), channel_id=1, source_target_pairs={{8,0},{16,8},{24,16},{32,24},{40,32},{48,40},{56,48},{64,56},{72,6... | collective-permute-start | bytes 983048 | tf_op jit(solution)/shard_map/ppermute | solution.py:20
  42.9 0.8 copy-start.14
  42.9 1.4 copy-start.16
  43.7 7.6 collective-permute-start.6
  44.3 7.0 collective-permute-start.7
  48.9 2.5 copy-start.15
  48.9 2.5 copy-start.17
  56.5 1.0 copy-start.3
  56.5 1.2 copy-start.5
  56.6 1.3 copy-start.8
  56.6 1.5 copy-start.10
  59.7 1.4 copy-start.13
  114.5 18.6 %copy-start.12 = (bf16[63,6144]{1,0:T(8,128)(2,1)S(1)}, bf16[63,6144]{1,0:T(8,128)(2,1)}, u32[]{:S(2)}) copy-start(bf16[63,6144]{1,0:T(8,128)(2,1)} %reshape.132) | copy-start | bytes 2322436
  114.5 20.2 %copy-start.19 = (f32[63,63]{0,1:T(8,128)S(1)}, f32[63,63]{0,1:T(8,128)}, u32[]{:S(2)}) copy-start(f32[63,63]{0,1:T(8,128)} %convolution_bitcast_fusion.11) | copy-start | bytes 47632
  235.2 2.9 collective-permute-start.8
  338.6 4.4 collective-permute-start.9
  443.6 2.9 collective-permute-start.10
  547.0 4.0 collective-permute-start.11
  651.6 6.9 collective-permute-start.12
  658.7 522.7 %copy-start.6 = (f32[63,6144]{1,0:T(8,128)S(1)}, f32[63,6144]{1,0:T(8,128)}, u32[]{:S(2)}) copy-start(f32[63,6144]{1,0:T(8,128)} %convert_element_type.115) | copy-start | bytes 4644868
  759.0 9.9 collective-permute-start.13
  869.5 2.9 collective-permute-start.14
  972.9 4.4 collective-permute-start.15
  1181.4 4.0 copy-start.11
where the time goes:
time: 1190 us
  matrix products  529 us (44%)
  loops' own time  424 us (36%)
  other arithmetic  94 us (8%)
  local copies, waits for them, and re-layouts  64.8 us (5%)
  waiting for transfers between devices  38.3 us (3%)
  starting transfers between devices  33.5 us (3%)
    dot_general x704, matrix products, matvec_rows(): jnp.dot(selector, matrix, precision=lax.Precision.HIGHEST, preferred_elem...  522 us
    another operation x9, loops' own time, cholesky_upper(): working, factor = lax.fori_loop(0, order, column_step, start)  424 us
    reshape x1, local copies, waits for them, and re-layouts, on_device(): velocity.reshape(3, coarse_x, 4, coarse_y, 4, coarse_z, 4)  53.3 us
    add x576, other arithmetic, column_step(): factor = factor + selector[:, None] * scaled_row[None, :]  49.4 us
  transfers between devices with their start and end apart: 16, of which 12 were waited for; matrix products, arithmetic and copies ran while one was open for 1% of the time, Pallas kernels for 0%

commit v1 on v0

v1 whole, which is shorter than its diff:
```python
import functools

import jax
import jax.numpy as jnp
from jax import lax
from jax.experimental import pallas as pl
from jax.experimental.pallas import tpu as pltpu
from jax.sharding import PartitionSpec as P

f32 = jnp.float32
bf16 = jnp.bfloat16
MESH = pl.DeviceIdType.MESH

time_step = 0.08
shear_friction_coefficient = 1.5
heat_conduction_coefficient = 1.5

X, Y, Z = 8, 64, 256
XP, YP = 12, 80
STEP_X = 2 * YP
SNAPS = 63
BLOCKS = 48
CHUNK = 32


def flat(ref):
    rows = 1
    for size in ref.shape[:-1]:
        rows *= size
    return ref.reshape(rows, 128)


def split3(value):
    high = value.astype(bf16)
    rest = value - high.astype(f32)
    middle = rest.astype(bf16)
    low = (rest - middle.astype(f32)).astype(bf16)
    return high, middle, low


def z_pair(pair, copied):
    low, high = pair
    lane = lax.broadcasted_iota(jnp.int32, low.shape, 1)
    last, first = lane == 127, lane == 0
    low_up, high_up = pltpu.roll(low, 127, 1), pltpu.roll(high, 127, 1)
    low_down, high_down = pltpu.roll(low, 1, 1), pltpu.roll(high, 1, 1)
    above, below = (high, low) if copied else (0.0, 0.0)
    up = (jnp.where(last, high_up, low_up), jnp.where(last, above, high_up))
    down = (jnp.where(first, below, low_down), jnp.where(first, low_down, high_down))
    return up, down


def primitives(state):
    inverse = 1.0 / state[0]
    return [state[1 + field] * inverse for field in range(4)]


def change(center, x_up, x_down, y_up, y_down, mx_up, mx_down, my_up, my_down, mz):
    up, down = z_pair(mz, False)
    result = [
        [
            (-0.5 * time_step) * ((mx_up[t] - mx_down[t]) + (my_up[t] - my_down[t]) + (up[t] - down[t]))
            for t in range(2)
        ]
    ]
    for field in range(4):
        rate = heat_conduction_coefficient if field == 3 else shear_friction_coefficient
        up, down = z_pair(center[field], field == 3)
        result.append(
            [
                (time_step * rate)
                * (
                    (x_up[field][t] + x_down[field][t])
                    + (y_up[field][t] + y_down[field][t])
                    + (up[t] + down[t])
                    - 6.0 * center[field][t]
                )
                for t in range(2)
            ]
        )
    return result


def change_rows(prim, state, x, row, count):
    def v(dx, dy):
        return [[prim[f, x + dx, t, pl.ds(row + dy, count), :] for t in range(2)] for f in range(4)]

    def s(field, dx, dy):
        return [state[field, x + dx, t, pl.ds(row + dy, count), :] for t in range(2)]

    return change(
        v(0, 0), v(1, 0), v(-1, 0), v(0, 1), v(0, -1),
        s(1, 1, 0), s(1, -1, 0), s(2, 0, 1), s(2, 0, -1), s(3, 0, 0),
    )


def primitive_layer(state, prim, x):
    for row in range(8, 8 + Y, CHUNK):
        for t in range(2):
            values = primitives([state[f, x, t, pl.ds(row, CHUNK), :] for f in range(5)])
            for f in range(4):
                prim[f, x, t, pl.ds(row, CHUNK), :] = values[f]


def first_layer(state, prim, state2, prim2, x):
    for row in range(8, 8 + Y, CHUNK):
        delta = change_rows(prim, state, x, row, CHUNK)
        for t in range(2):
            new = [state[f, x, t, pl.ds(row, CHUNK), :] + delta[f][t] for f in range(5)]
            values = primitives(new)
            for f in range(5):
                state2[f, x, t, pl.ds(row, CHUNK), :] = new[f]
            for f in range(4):
                prim2[f, x, t, pl.ds(row, CHUNK), :] = values[f]


def second_layer(state, state2, prim2, updated, sums, x):
    for row in range(8, 8 + Y, CHUNK):
        delta = change_rows(prim2, state2, x, row, CHUNK)
        for t in range(2):
            new = [
                0.5 * state[f, x, t, pl.ds(row, CHUNK), :]
                + 0.5 * (state2[f, x, t, pl.ds(row, CHUNK), :] + delta[f][t])
                for f in range(5)
            ]
            inverse = 1.0 / new[0]
            for f in range(5):
                updated[f, x - 2, t, pl.ds(row - 8, CHUNK), :] = new[f]
            for c in range(3):
                sums[c, (x - 2) // 4, t, pl.ds(row - 8, CHUNK), :] += new[1 + c] * inverse


def sheet(field, tile, row, dx=0):
    return pl.ds(((field * XP + 2 + dx) * 2 + tile) * YP + row, X, stride=STEP_X)


def place_rows(state, prim, y_in, side):
    row = 7 if side == 0 else 72
    flat_state, flat_prim = flat(state), flat(prim)
    for t in range(2):
        near = [y_in[side, f, 0, t] for f in range(5)]
        values = primitives(near)
        for f in range(4):
            flat_prim[sheet(f, t, row), :] = values[f]
        for f in (1, 2):
            flat_state[sheet(f, t, row), :] = near[f]


def place_corner(state, prim, corner_in, side_x, side_y):
    x = 1 if side_x == 0 else 10
    row = 7 if side_y == 0 else 72
    for t in range(2):
        values = corner_in[side_x, side_y, t]
        inverse = 1.0 / values[0:1]
        for f in range(4):
            prim[f, x, t, pl.ds(row, 1), :] = values[1 + f : 2 + f] * inverse
        for f in (1, 2):
            state[f, x, t, pl.ds(row, 1), :] = values[f : f + 1]


def edge_rows(state, prim, state2, prim2, y_in, side):
    row, own = (7, 8) if side == 0 else (72, 71)
    flat_state, flat_prim = flat(state), flat(prim)
    flat_state2, flat_prim2 = flat(state2), flat(prim2)

    def v(at, dx):
        return [[flat_prim[sheet(f, t, at, dx), :] for t in range(2)] for f in range(4)]

    def s(field, at, dx):
        return [flat_state[sheet(field, t, at, dx), :] for t in range(2)]

    near = [[y_in[side, f, 0, t] for f in range(5)] for t in range(2)]
    far = [primitives([y_in[side, f, 1, t] for f in range(5)]) for t in range(2)]
    far = [[far[t][f] for t in range(2)] for f in range(4)]
    far_my = [y_in[side, 2, 1, t] for t in range(2)]
    inner, inner_my = v(own, 0), s(2, own, 0)
    y_up, y_down, my_up, my_down = (
        (inner, far, inner_my, far_my) if side == 0 else (far, inner, far_my, inner_my)
    )
    delta = change(
        v(row, 0), v(row, 1), v(row, -1), y_up, y_down,
        s(1, row, 1), s(1, row, -1), my_up, my_down, [near[t][3] for t in range(2)],
    )
    for t in range(2):
        new = [near[t][f] + delta[f][t] for f in range(5)]
        values = primitives(new)
        for f in range(4):
            flat_prim2[sheet(f, t, row), :] = values[f]
        flat_state2[sheet(2, t, row), :] = new[2]


def eliminate(rows):
    sub = lax.broadcasted_iota(jnp.int32, (8, 128), 0)
    for k in range(SNAPS):
        block, at = divmod(k, 8)
        row = jnp.broadcast_to(rows[block][at : at + 1, :], (8, 128))
        pivot = jnp.broadcast_to(row[:, k : k + 1], (8, 128))
        scaled = row * (1.0 / pivot)
        for b in range(block, 8):
            column = jnp.broadcast_to(rows[b][:, k : k + 1], (8, 128))
            if b == block:
                column = jnp.where(sub > at, column, 0.0)
            rows[b] = rows[b] - column * scaled
    return rows


def kernel(
    rows_all, sizes,
    density, momentum, energy, snapshots,
    out_density, out_momentum, out_energy, out_factor, out_modes,
    state, prim, state2, prim2, updated, sums,
    y_out, y_in, corner_out, corner_in,
    snap_in, snap_f, snap_b, modes, factor_v, coarse,
    gram, gram_part, gram_z, gram_y, gram_all, gram_sums,
    dot_gy, dot_z, dot_y, dot_sums,
    load_sem, store_sem,
    x_send, x_recv, y_send, y_recv, corner_send, corner_recv,
    gram_send, gram_recv, dot_send, dot_recv,
):
    n_gx, n_gy, n_y = sizes
    n_z = n_gx // n_y
    gx, gy = lax.axis_index("gx"), lax.axis_index("gy")
    iz, iy = lax.div(gx, n_y), lax.rem(gx, n_y)

    def moved(dx, dy):
        return {"gx": lax.rem(gx + dx + n_gx, n_gx), "gy": lax.rem(gy + dy + n_gy, n_gy)}

    def on_gy(i):
        return {"gx": gx, "gy": i}

    def on_z(i):
        return {"gx": i * n_y + iy, "gy": gy}

    def on_y(i):
        return {"gx": iz * n_y + i, "gy": gy}

    loads = []
    for t in range(2):
        lanes, rows = pl.ds(128 * t, 128), pl.ds(8, Y)
        loads += [
            pltpu.make_async_copy(density.at[:, :, lanes], state.at[0, pl.ds(2, X), t, rows, :], load_sem.at[3 * t]),
            pltpu.make_async_copy(
                momentum.at[:, :, :, lanes], state.at[pl.ds(1, 3), pl.ds(2, X), t, rows, :], load_sem.at[3 * t + 1]
            ),
            pltpu.make_async_copy(energy.at[:, :, lanes], state.at[4, pl.ds(2, X), t, rows, :], load_sem.at[3 * t + 2]),
        ]
    load_snapshots = pltpu.make_async_copy(snapshots, snap_in, load_sem.at[6])
    for copy in loads:
        copy.start()
    load_snapshots.start()

    barrier = pltpu.get_barrier_semaphore()
    greeted = [moved(dx, dy) for dx in (-1, 1) for dy in (-1, 0, 1)]
    greeted += [on_gy(lax.rem(gy + d, n_gy)) for d in range(1, n_gy)]
    greeted += [on_z(lax.rem(iz + d, n_z)) for d in range(1, n_z)]
    greeted += [on_y(lax.rem(iy + d, n_y)) for d in range(1, n_y)]
    for device in greeted:
        pl.semaphore_signal(barrier, inc=1, device_id=device, device_id_type=MESH)
    pl.semaphore_wait(barrier, len(greeted))

    def remote(source, target, send_sem, recv_sem, device):
        return pltpu.make_async_remote_copy(
            src_ref=source, dst_ref=target, send_sem=send_sem, recv_sem=recv_sem, device_id=device, device_id_type=MESH
        )

    def x_copies(layer):
        copies = []
        for side in range(2):
            source, target = (X - 1 - layer, 1 - layer) if side == 0 else (layer, 10 + layer)
            device = moved(1, 0) if side == 0 else moved(-1, 0)
            for t in range(2):
                lanes, rows = pl.ds(128 * t, 128), pl.ds(8, Y)
                at = ((layer * 2 + side) * 2 + t) * 3
                copies += [
                    remote(
                        density.at[source, :, lanes], state.at[0, target, t, rows, :],
                        x_send.at[at], x_recv.at[at], device,
                    ),
                    remote(
                        momentum.at[:, source, :, lanes], state.at[pl.ds(1, 3), target, t, rows, :],
                        x_send.at[at + 1], x_recv.at[at + 1], device,
                    ),
                    remote(
                        energy.at[source, :, lanes], state.at[4, target, t, rows, :],
                        x_send.at[at + 2], x_recv.at[at + 2], device,
                    ),
                ]
        return copies

    near_copies, far_copies = x_copies(0), x_copies(1)
    for copy in near_copies:
        copy.start()

    for copy in loads:
        copy.wait()
    flat_state = flat(state)
    for side in range(2):
        for f in range(5):
            for far in range(2):
                y = Y - 1 - far if side == 0 else far
                for t in range(2):
                    y_out[side, f, far, t] = flat_state[sheet(f, t, 8 + y), :]
    y_copies = [
        remote(y_out.at[side], y_in.at[side], y_send.at[side], y_recv.at[side], moved(0, 1 - 2 * side))
        for side in range(2)
    ]
    for copy in y_copies:
        copy.start()
    corner_out[...] = jnp.zeros_like(corner_out)
    corner_copies = []
    for side_x in range(2):
        for side_y in range(2):
            x, y = (X - 1) * (1 - side_x), (Y - 1) * (1 - side_y)
            for t in range(2):
                start = ((2 + x) * 2 + t) * YP + 8 + y
                corner_out[side_x, side_y, t, 0:5] = flat_state[pl.ds(start, 5, stride=XP * STEP_X), :]
            at = side_x * 2 + side_y
            corner_copies.append(
                remote(
                    corner_out.at[side_x, side_y], corner_in.at[side_x, side_y],
                    corner_send.at[at], corner_recv.at[at], moved(1 - 2 * side_x, 1 - 2 * side_y),
                )
            )
    for copy in corner_copies:
        copy.start()

    load_snapshots.wait()
    for c in range(3):
        snap_f[0:SNAPS, c] = snap_in[:, c].astype(f32)
    snap_f[SNAPS] = jnp.zeros((3, 16, 128), f32)
    flat_snap, flat_modes = flat(snap_f), flat(modes)

    def gram_step(i, total):
        pair = jnp.concatenate([flat_snap[pl.ds(2 * i + half, 64, stride=BLOCKS), :] for half in range(2)], axis=1)
        pair = pair.astype(bf16)
        snap_b[i] = pair
        return total + lax.dot_general(pair, pair, (((1,), (1,)), ((), ())), preferred_element_type=f32)

    local = lax.fori_loop(0, BLOCKS // 2, gram_step, jnp.zeros((64, 64), f32))
    local = jnp.concatenate([local, jnp.zeros((64, 64), f32)], axis=1)
    for b in range(8):
        gram[b] = local[8 * b : 8 * b + 8]

    def exchange(sources, target, me, count, device_of, send, recv, first):
        copies = []
        for d in range(1, count):
            peer = lax.rem(me + d, count)
            copies.append(
                remote(sources(peer), target.at[me], send.at[first + d], recv.at[first + d], device_of(peer))
            )
        for copy in copies:
            copy.start()
        return copies

    def total(ref, count):
        value = ref[0]
        for i in range(1, count):
            value = value + ref[i]
        return value

    copies = exchange(lambda peer: gram.at[peer], gram_part, gy, n_gy, on_gy, gram_send, gram_recv, 0)
    gram_part[gy] = gram[gy]

    def loop(start, stop, step):
        lax.fori_loop(start, stop, lambda x, _: (step(x), 0)[1], 0)

    loop(2, 2 + X, lambda x: primitive_layer(state, prim, x))
    for copy in copies:
        copy.wait()
    gram_sums[0] = total(gram_part, n_gy)
    copies = exchange(lambda peer: gram_sums.at[0], gram_z, iz, n_z, on_z, gram_send, gram_recv, 8)
    gram_z[iz] = gram_sums[0]
    for copy in y_copies:
        copy.wait()
    for side in range(2):
        place_rows(state, prim, y_in, side)
    loop(3, 1 + X, lambda x: first_layer(state, prim, state2, prim2, x))
    for copy in copies:
        copy.wait()
    gram_sums[1] = total(gram_z, n_z)
    copies = exchange(lambda peer: gram_sums.at[1], gram_y, iy, n_y, on_y, gram_send, gram_recv, 16)
    gram_y[iy] = gram_sums[1]
    for copy in far_copies:
        copy.start()
    for copy in copies:
        copy.wait()
    gram_sums[2] = total(gram_y, n_y)
    copies = exchange(lambda peer: gram_sums.at[2], gram_all, gy, n_gy, on_gy, gram_send, gram_recv, 24)
    gram_all[gy] = gram_sums[2]

    sums[...] = jnp.zeros_like(sums)
    for copy in near_copies + corner_copies:
        copy.wait()
    loop(0, 2, lambda i: primitive_layer(state, prim, 1 + 9 * i))
    for side_x in range(2):
        for side_y in range(2):
            place_corner(state, prim, corner_in, side_x, side_y)
    loop(0, 2, lambda i: first_layer(state, prim, state2, prim2, 2 + 7 * i))
    for side in range(2):
        edge_rows(state, prim, state2, prim2, y_in, side)
    for copy in copies:
        copy.wait()

    lane = lax.broadcasted_iota(jnp.int32, (8, 128), 1)
    sub = lax.broadcasted_iota(jnp.int32, (8, 128), 0)
    blocks = []
    for b in range(8):
        row = sub + 8 * b
        known = (row < SNAPS) & (lane < SNAPS)
        unit = ((lane == row) & (row == SNAPS)) | (lane == row + 64)
        blocks.append(jnp.where(known, gram_all[b] / rows_all, jnp.where(unit, 1.0, 0.0)))
    blocks = eliminate(blocks)
    lower = []
    for b in range(8):
        row = sub + 8 * b
        diagonal = jnp.sum(jnp.where(lane == row, blocks[b], 0.0), axis=1, keepdims=True)
        scaled = blocks[b] * (1.0 / jnp.sqrt(diagonal))
        factor_v[b] = jnp.where((lane >= row) & (lane < SNAPS), scaled, 0.0)
        lower.append(jnp.where(row < SNAPS, pltpu.roll(scaled, 64, 1), 0.0))
    lower = jnp.concatenate(lower, axis=0)[:, :64]
    stacked = jnp.concatenate(split3(lower), axis=0)

    def modes_step(i, carry):
        parts = jnp.dot(stacked, snap_b[i], preferred_element_type=f32)
        both = parts[0:64] + (parts[64:128] + parts[128:192])
        for half in range(2):
            flat_modes[pl.ds(2 * i + half, 64, stride=BLOCKS), :] = both[:, 128 * half : 128 * half + 128]
        return carry

    lax.fori_loop(0, BLOCKS // 2, modes_step, 0)
    store_modes = pltpu.make_async_copy(
        flat_modes.at[pl.ds(0, SNAPS * BLOCKS)], out_modes.at[pl.ds(0, SNAPS * BLOCKS)], store_sem.at[6]
    )
    store_modes.start()

    loop(4, X, lambda x: second_layer(state, state2, prim2, updated, sums, x))
    for copy in far_copies:
        copy.wait()
    loop(0, 2, lambda i: primitive_layer(state, prim, 11 * i))
    loop(0, 2, lambda i: first_layer(state, prim, state2, prim2, 1 + 9 * i))
    loop(2, 4, lambda x: second_layer(state, state2, prim2, updated, sums, x))
    loop(X, 2 + X, lambda x: second_layer(state, state2, prim2, updated, sums, x))
    stores = [store_modes]
    for t in range(2):
        lanes = pl.ds(128 * t, 128)
        stores += [
            pltpu.make_async_copy(updated.at[0, :, t], out_density.at[:, :, lanes], store_sem.at[3 * t]),
            pltpu.make_async_copy(updated.at[pl.ds(1, 3), :, t], out_momentum.at[:, :, :, lanes], store_sem.at[3 * t + 1]),
            pltpu.make_async_copy(updated.at[4, :, t], out_energy.at[:, :, lanes], store_sem.at[3 * t + 2]),
        ]
    for copy in stores[1:]:
        copy.start()

    flat_sums = flat(sums)
    columns = []
    for half in range(2):
        for t in range(2):
            parts = []
            for c in range(6):
                start = (c * 2 + t) * Y + 4 * half
                part = flat_sums[pl.ds(start, 8, stride=8), :]
                for k in range(1, 4):
                    part = part + flat_sums[pl.ds(start + k, 8, stride=8), :]
                parts.append(part)
            columns.append(jnp.concatenate(parts, axis=0))
    fine = jnp.concatenate(columns, axis=1)
    source = lax.broadcasted_iota(jnp.int32, (512, 128), 0)
    target = lax.broadcasted_iota(jnp.int32, (512, 128), 1)
    gather = jnp.where(lax.shift_right_logical(source, 2) == target, 1.0 / 64.0, 0.0).astype(bf16)
    means = sum(jnp.dot(part, gather, preferred_element_type=f32) for part in split3(fine))
    for c in range(3):
        for half in range(2):
            first = (2 * c + half) * 8
            coarse[pl.ds(16 * c + half, 8, stride=2), :] = means[first : first + 8]

    def dot_step(i, acc):
        for part in range(4):
            b = 4 * i + part
            acc = acc + flat_modes[pl.ds(b, 64, stride=BLOCKS), :] * coarse[pl.ds(b, 1), :]
        return acc

    acc = lax.fori_loop(0, BLOCKS // 4, dot_step, jnp.zeros((64, 128), f32))
    squares = jnp.sum(coarse[...] * coarse[...], axis=0, keepdims=True)
    acc = jnp.where(lax.broadcasted_iota(jnp.int32, (64, 128), 0) == SNAPS, squares, acc)
    ones = jnp.ones((8, 128), bf16)
    products = sum(
        lax.dot_general(ones, part, (((1,), (1,)), ((), ())), preferred_element_type=f32) for part in split3(acc)
    )
    dot_sums[0] = jnp.concatenate([products, jnp.zeros((8, 64), f32)], axis=1)
    stages = ((dot_gy, gy, n_gy, on_gy, 0), (dot_z, iz, n_z, on_z, 8), (dot_y, iy, n_y, on_y, 16))
    for stage, (target, me, count, device_of, first) in enumerate(stages):
        copies = exchange(lambda peer: dot_sums.at[stage], target, me, count, device_of, dot_send, dot_recv, first)
        target[me] = dot_sums[stage]
        for copy in copies:
            copy.wait()
        dot_sums[stage + 1] = total(target, count)
    share = dot_sums[3] / rows_all

    rest = jnp.where(lane < SNAPS, share, 0.0)
    norm = jnp.sum(jnp.where(lane == SNAPS, share, 0.0), axis=1, keepdims=True)
    last = jnp.sqrt(norm - jnp.sum(rest * rest, axis=1, keepdims=True))
    for b in range(8):
        row = sub + 8 * b
        column = jnp.sum(jnp.where(lane == row, rest, 0.0), axis=1, keepdims=True)
        column = jnp.where(row == SNAPS, last, column)
        out_factor[8 * b : 8 * b + 8, :] = jnp.where(lane == SNAPS, column, factor_v[b])[:, :64]
    mode = [coarse[8 * i : 8 * i + 8, :] for i in range(6)]
    for m in range(SNAPS):
        weight = jnp.broadcast_to(rest[:, m : m + 1], (8, 128))
        for i in range(6):
            mode[i] = mode[i] - weight * flat_modes[BLOCKS * m + 8 * i : BLOCKS * m + 8 * i + 8, :]
    scale = 1.0 / last
    for i in range(6):
        flat_modes[BLOCKS * SNAPS + 8 * i : BLOCKS * SNAPS + 8 * i + 8, :] = mode[i] * scale
    store_last = pltpu.make_async_copy(
        flat_modes.at[pl.ds(SNAPS * BLOCKS, BLOCKS)], out_modes.at[pl.ds(SNAPS * BLOCKS, BLOCKS)], store_sem.at[7]
    )
    store_last.start()
    for copy in stores + [store_last]:
        copy.wait()


def solution(mesh):
    n_gx, n_gy = mesh.shape["gx"], mesh.shape["gy"]
    n_y = 4
    n_z = n_gx // n_y

    def on_device(density, momentum, energy, snapshots):
        rows_all = 6144 * n_gx * n_gy
        snapshots = snapshots.reshape(SNAPS, 3, 2, 8, 128).transpose(0, 1, 3, 2, 4).reshape(SNAPS, 3, 16, 128)
        anywhere = pl.BlockSpec(memory_space=pl.ANY)
        vmem = pl.BlockSpec(memory_space=pltpu.VMEM)
        dma = pltpu.SemaphoreType.DMA
        new_density, new_momentum, new_energy, factor, modes = pl.pallas_call(
            functools.partial(kernel, float(rows_all), (n_gx, n_gy, n_y)),
            name="sections_and_modes",
            in_specs=[anywhere] * 4,
            out_specs=(anywhere, anywhere, anywhere, vmem, anywhere),
            out_shape=(
                jax.ShapeDtypeStruct((X, Y, Z), f32),
                jax.ShapeDtypeStruct((3, X, Y, Z), f32),
                jax.ShapeDtypeStruct((X, Y, Z), f32),
                jax.ShapeDtypeStruct((64, 64), f32),
                jax.ShapeDtypeStruct((64 * BLOCKS, 128), f32),
            ),
            scratch_shapes=[
                pltpu.VMEM((5, XP, 2, YP, 128), f32),
                pltpu.VMEM((4, XP, 2, YP, 128), f32),
                pltpu.VMEM((5, XP, 2, YP, 128), f32),
                pltpu.VMEM((4, XP, 2, YP, 128), f32),
                pltpu.VMEM((5, X, 2, Y, 128), f32),
                pltpu.VMEM((3, 2, 2, Y, 128), f32),
                pltpu.VMEM((2, 5, 2, 2, 8, 128), f32),
                pltpu.VMEM((2, 5, 2, 2, 8, 128), f32),
                pltpu.VMEM((2, 2, 2, 8, 128), f32),
                pltpu.VMEM((2, 2, 2, 8, 128), f32),
                pltpu.VMEM((SNAPS, 3, 16, 128), bf16),
                pltpu.VMEM((64, 3, 16, 128), f32),
                pltpu.VMEM((BLOCKS // 2, 64, 256), bf16),
                pltpu.VMEM((64, 3, 16, 128), f32),
                pltpu.VMEM((8, 8, 128), f32),
                pltpu.VMEM((BLOCKS, 128), f32),
                pltpu.VMEM((8, 8, 128), f32),
                pltpu.VMEM((n_gy, 8, 128), f32),
                pltpu.VMEM((n_z, 8, 128), f32),
                pltpu.VMEM((n_y, 8, 128), f32),
                pltpu.VMEM((8, 8, 128), f32),
                pltpu.VMEM((3, 8, 128), f32),
                pltpu.VMEM((n_gy, 8, 128), f32),
                pltpu.VMEM((n_z, 8, 128), f32),
                pltpu.VMEM((n_y, 8, 128), f32),
                pltpu.VMEM((4, 8, 128), f32),
                dma((7,)),
                dma((8,)),
                dma((24,)),
                dma((24,)),
                dma((2,)),
                dma((2,)),
                dma((4,)),
                dma((4,)),
                dma((32,)),
                dma((32,)),
                dma((24,)),
                dma((24,)),
            ],
            compiler_params=pltpu.CompilerParams(
                collective_id=0, has_side_effects=True, vmem_limit_bytes=32 * 2**20
            ),
        )(density, momentum, energy, snapshots)
        modes = modes.reshape(64, 3, 8, 2, 128).transpose(0, 1, 3, 2, 4).reshape(64, 3, 2, 1024)
        return new_density, new_momentum, new_energy, factor, modes

    placed = (
        P("gx", "gy", None),
        P(None, "gx", "gy", None),
        P("gx", "gy", None),
        P(None, None, "gx", "gy"),
    )
    return jax.shard_map(
        on_device,
        mesh=mesh,
        in_specs=placed,
        out_specs=(
            P("gx", "gy", None),
            P(None, "gx", "gy", None),
            P("gx", "gy", None),
            P(),
            P(None, None, "gx", "gy"),
        ),
        check_vma=False,
    )
```

time: 1190 us -> 68.8 us (0.06)
  matrix products: 529 us -> 0 us
  loops' own time: 424 us -> 0 us
  other arithmetic: 94 us -> 0 us
  Pallas kernels: 0 us -> 58.8 us
  local copies, waits for them, and re-layouts: 64.8 us -> 9.1 us
  waiting for transfers between devices: 38.3 us -> 0 us
  starting transfers between devices: 33.5 us -> 0 us
    dot_general x723 -> x0, matrix products: 529 us -> none  [the longest x704 522 us: matvec_rows(): jnp.dot(selector, matrix, precision=lax.Precision.HIGHEST, preferred_elem...]
    another operation x10 -> x0, loops' own time: 424 us -> none  [the longest x9 424 us: cholesky_upper(): working, factor = lax.fori_loop(0, order, column_step, start)]
    reshape x3 -> x0, local copies, waits for them, and re-layouts: 59 us -> none  [the longest x1 53.3 us: on_device(): velocity.reshape(3, coarse_x, 4, coarse_y, 4, coarse_z, 4)]
    pallas_call x0 -> x1, Pallas kernels: none -> 58.8 us  [on_device(): pl.pallas_call(functools.partial(kernel, float(rows_all), (n_gx, n_gy, n_...]
    add x642 -> x0, other arithmetic: 55.6 us -> none  [the longest x576 49.4 us: column_step(): factor = factor + selector[:, None] * scaled_row[None, :]]
    ppermute x16 -> x0, waiting for transfers between devices: 38.3 us -> none  [the longest x8 19.9 us: from_partner(): return lax.ppermute(value, axis, pairs)]
    ppermute x16 -> x0, starting transfers between devices: 33.5 us -> none  [the longest x8 16 us: from_partner(): return lax.ppermute(value, axis, pairs)]
    reduce_sum x1 -> x0, other arithmetic: 17.9 us -> none  [on_device(): velocity.reshape(3, coarse_x, 4, coarse_y, 4, coarse_z, 4)]
  transfers between devices with their start and end apart: 16 -> 0, of which waited for: 12 -> 0; matrix products, arithmetic and copies ran while one was open for 1% -> 0% of each run, Pallas kernels for 0% -> 0%
where the time goes in v1:
time: 68.8 us; the launch traced here: 68.6 us
  Pallas kernels  58.8 us (85%)
  local copies, waits for them, and re-layouts  9.1 us (13%)
    pallas_call x1, Pallas kernels, on_device(): pl.pallas_call(functools.partial(kernel, float(rows_all), (n_gx, n_gy, n_...  58.8 us
    unnamed x13, local copies, waits for them, and re-layouts  9.1 us

profile of v1, /device:TPU:1, one launch (start us, length us, event | category | flops | bytes accessed | tf_op | source)
XLA Modules:
  0.0 68.6 jit_solution(14795277834357575095)
XLA Ops:
  0.6 0.0 copy-start
  0.6 1.4 %copy-done = f32[3,8,64,256]{3,2,1,0:T(8,128)S(1)} copy-done((f32[3,8,64,256]{3,2,1,0:T(8,128)S(1)}, f32[3,8,64,256]{3,2,1,0:T(8,128)}, u32[]{:S(2)}) %copy-start) | copy-done | bytes 1572888
  2.0 0.0 copy-start.1
  2.0 1.1 %copy-done.1 = bf16[63,3,2,1024]{3,2,1,0:T(2,128)(2,1)S(1)} copy-done((bf16[63,3,2,1024]{3,2,1,0:T(2,128)(2,1)S(1)}, bf16[63,3,2,1024]{3,2,1,0:T(2,128)(2,1)}, u32[]{:S(2)}) %copy-start.1) | copy-done | bytes 774168
  3.2 0.0 copy-start.2
  3.2 1.0 %copy-done.2 = f32[8,64,256]{2,1,0:T(8,128)S(1)} copy-done((f32[8,64,256]{2,1,0:T(8,128)S(1)}, f32[8,64,256]{2,1,0:T(8,128)}, u32[]{:S(2)}) %copy-start.2) | copy-done | bytes 524312
  4.2 0.0 copy-start.3
  4.2 1.0 %copy-done.3 = f32[8,64,256]{2,1,0:T(8,128)S(1)} copy-done((f32[8,64,256]{2,1,0:T(8,128)S(1)}, f32[8,64,256]{2,1,0:T(8,128)}, u32[]{:S(2)}) %copy-start.3) | copy-done | bytes 524312
  5.3 58.8 %sections_and_modes.1 = (f32[8,64,256]{2,1,0:T(8,128)S(1)}, f32[3,8,64,256]{3,2,1,0:T(8,128)S(1)}, f32[8,64,256]{2,1,0:T(8,128)S(1)}, f32[64,64]{1,0:T(8,128)S(1)}, f32[3072,128]{1,0:T(8,128)S(1)}) custom-call(f32[8,64,256]{2,1,0:T(8,128)S(1)} %copy-done.2, f32[3,8,64,256]{3,2,1,0:T(8,128)S(1)} %copy-done, f32[8,64,256]{2,1,0:T(8,128)S(1)} %copy-done.3, ...), custom_call_target="tpu_custom_call" | custom-call | tf_op jit(solution)/shard_map/sections_and_modes/pallas_call | solution.py:534
  64.1 0.8 %copy.16 = f32[8,64,256]{2,1,0:T(8,128)} copy(f32[8,64,256]{2,1,0:T(8,128)S(1)} %get-tuple-element.20) | data formatting | bytes 1048576
  64.9 1.1 %copy.17 = f32[3,8,64,256]{3,2,1,0:T(8,128)} copy(f32[3,8,64,256]{3,2,1,0:T(8,128)S(1)} %get-tuple-element.21) | data formatting | bytes 3145728
  66.0 0.8 %copy.18 = f32[8,64,256]{2,1,0:T(8,128)} copy(f32[8,64,256]{2,1,0:T(8,128)S(1)} %get-tuple-element.22) | data formatting | bytes 1048576
  66.8 0.6 copy.19
  67.4 1.1 %copy.20 = f32[64,3,2,1024]{3,2,1,0:T(2,128)} copy(f32[64,3,2,1024]{3,2,1,0:T(2,128)S(1)} %bitcast.10) | data formatting | bytes 3145728
Async XLA Ops:
  0.6 1.4 %copy-start = (f32[3,8,64,256]{3,2,1,0:T(8,128)S(1)}, f32[3,8,64,256]{3,2,1,0:T(8,128)}, u32[]{:S(2)}) copy-start(f32[3,8,64,256]{3,2,1,0:T(8,128)} %momentum.1) | copy-start | bytes 4718596
  2.0 1.1 %copy-start.1 = (bf16[63,3,2,1024]{3,2,1,0:T(2,128)(2,1)S(1)}, bf16[63,3,2,1024]{3,2,1,0:T(2,128)(2,1)}, u32[]{:S(2)}) copy-start(bf16[63,3,2,1024]{3,2,1,0:T(2,128)(2,1)} %param.7) | copy-start | bytes 2322436
  3.2 1.0 %copy-start.2 = (f32[8,64,256]{2,1,0:T(8,128)S(1)}, f32[8,64,256]{2,1,0:T(8,128)}, u32[]{:S(2)}) copy-start(f32[8,64,256]{2,1,0:T(8,128)} %density.1) | copy-start | bytes 1572868
  4.2 1.0 %copy-start.3 = (f32[8,64,256]{2,1,0:T(8,128)S(1)}, f32[8,64,256]{2,1,0:T(8,128)}, u32[]{:S(2)}) copy-start(f32[8,64,256]{2,1,0:T(8,128)} %energy.1) | copy-start | bytes 1572868

commit v2 on v1

--- a/solution.py
+++ b/solution.py
@@ -21,6 +21,9 @@
 SNAPS = 63
 BLOCKS = 48
 CHUNK = 32
+UNROLL = 4
+FAR_AT = 0
+SPLIT = 24
 
 
 def flat(ref):
@@ -189,18 +192,33 @@
         flat_state2[sheet(2, t, row), :] = new[2]
 
 
-def eliminate(rows):
+def eliminate(rows, first, stop):
     sub = lax.broadcasted_iota(jnp.int32, (8, 128), 0)
-    for k in range(SNAPS):
+
+    def along_lanes(value, k):
+        return jnp.broadcast_to(value[:, k : k + 1], (8, 128))
+
+    def along_rows(value, k):
+        return jnp.broadcast_to(value[k : k + 1, :], (8, 128))
+
+    for k in range(first, stop, 2):
         block, at = divmod(k, 8)
-        row = jnp.broadcast_to(rows[block][at : at + 1, :], (8, 128))
-        pivot = jnp.broadcast_to(row[:, k : k + 1], (8, 128))
-        scaled = row * (1.0 / pivot)
+        left = {b: along_lanes(rows[b], k) for b in range(block, 8)}
+        right = {b: along_lanes(rows[b], k + 1) for b in range(block, 8)}
+        cross = along_rows(left[block], at + 1)
+        inverse = 1.0 / along_rows(left[block], at)
+        ratio = cross * inverse
+        pivot = along_rows(right[block], at + 1) - ratio * cross
+        row = along_rows(rows[block], at)
+        next_row = along_rows(rows[block], at + 1) - ratio * row
+        row = row * inverse
+        next_row = next_row * (1.0 / pivot)
         for b in range(block, 8):
-            column = jnp.broadcast_to(rows[b][:, k : k + 1], (8, 128))
+            first_column, second_column = left[b], right[b] - ratio * left[b]
             if b == block:
-                column = jnp.where(sub > at, column, 0.0)
-            rows[b] = rows[b] - column * scaled
+                first_column = jnp.where(sub > at, first_column, 0.0)
+                second_column = jnp.where(sub > at + 1, second_column, 0.0)
+            rows[b] = rows[b] - first_column * row - second_column * next_row
     return rows
 
 
@@ -210,7 +228,7 @@
     out_density, out_momentum, out_energy, out_factor, out_modes,
     state, prim, state2, prim2, updated, sums,
     y_out, y_in, corner_out, corner_in,
-    snap_in, snap_f, snap_b, modes, factor_v, coarse,
+    snap_in, snap_f, snap_b, modes, factor_v, lower_v, coarse,
     gram, gram_part, gram_z, gram_y, gram_all, gram_sums,
     dot_gy, dot_z, dot_y, dot_sums,
     load_sem, store_sem,
@@ -287,12 +305,59 @@
                 ]
         return copies
 
+    def start(copies):
+        for copy in copies:
+            copy.start()
+
+    def wait(copies):
+        for copy in copies:
+            copy.wait()
+
+    def loop(first, stop, step):
+        lax.fori_loop(first, stop, lambda x, _: (step(x), 0)[1], 0)
+
+    def exchange(sources, target, me, count, device_of, send, recv, first):
+        copies = []
+        for d in sorted(range(1, count), key=lambda d: -min(d, count - d)):
+            peer = lax.rem(me + d, count)
+            copies.append(
+                remote(sources(peer), target.at[me], send.at[first + d], recv.at[first + d], device_of(peer))
+            )
+        start(copies)
+        return copies
+
+    def total(ref, count):
+        value = ref[0]
+        for i in range(1, count):
+            value = value + ref[i]
+        return value
+
     near_copies, far_copies = x_copies(0), x_copies(1)
-    for copy in near_copies:
-        copy.start()
-
-    for copy in loads:
-        copy.wait()
+    start(near_copies)
+
+    load_snapshots.wait()
+    for c in range(3):
+        snap_f[0:SNAPS, c] = snap_in[:, c].astype(f32)
+    snap_f[SNAPS] = jnp.zeros((3, 16, 128), f32)
+    flat_snap, flat_modes = flat(snap_f), flat(modes)
+
+    def gram_step(i, value):
+        for part in range(UNROLL):
+            at = UNROLL * i + part
+            pair = [flat_snap[pl.ds(2 * at + half, 64, stride=BLOCKS), :] for half in range(2)]
+            pair = jnp.concatenate(pair, axis=1).astype(bf16)
+            snap_b[at] = pair
+            value = value + lax.dot_general(pair, pair, (((1,), (1,)), ((), ())), preferred_element_type=f32)
+        return value
+
+    local = lax.fori_loop(0, BLOCKS // 2 // UNROLL, gram_step, jnp.zeros((64, 64), f32))
+    local = jnp.concatenate([local, jnp.zeros((64, 64), f32)], axis=1)
+    for b in range(8):
+        gram[b] = local[8 * b : 8 * b + 8]
+    scatter = exchange(lambda peer: gram.at[peer], gram_part, gy, n_gy, on_gy, gram_send, gram_recv, 0)
+    gram_part[gy] = gram[gy]
+
+    wait(loads)
     flat_state = flat(state)
     for side in range(2):
         for f in range(5):
@@ -304,16 +369,15 @@
         remote(y_out.at[side], y_in.at[side], y_send.at[side], y_recv.at[side], moved(0, 1 - 2 * side))
         for side in range(2)
     ]
-    for copy in y_copies:
-        copy.start()
+    start(y_copies)
     corner_out[...] = jnp.zeros_like(corner_out)
     corner_copies = []
     for side_x in range(2):
         for side_y in range(2):
             x, y = (X - 1) * (1 - side_x), (Y - 1) * (1 - side_y)
             for t in range(2):
-                start = ((2 + x) * 2 + t) * YP + 8 + y
-                corner_out[side_x, side_y, t, 0:5] = flat_state[pl.ds(start, 5, stride=XP * STEP_X), :]
+                begin = ((2 + x) * 2 + t) * YP + 8 + y
+                corner_out[side_x, side_y, t, 0:5] = flat_state[pl.ds(begin, 5, stride=XP * STEP_X), :]
             at = side_x * 2 + side_y
             corner_copies.append(
                 remote(
@@ -321,76 +385,29 @@
                     corner_send.at[at], corner_recv.at[at], moved(1 - 2 * side_x, 1 - 2 * side_y),
                 )
             )
-    for copy in corner_copies:
-        copy.start()
-
-    load_snapshots.wait()
-    for c in range(3):
-        snap_f[0:SNAPS, c] = snap_in[:, c].astype(f32)
-    snap_f[SNAPS] = jnp.zeros((3, 16, 128), f32)
-    flat_snap, flat_modes = flat(snap_f), flat(modes)
-
-    def gram_step(i, total):
-        pair = jnp.concatenate([flat_snap[pl.ds(2 * i + half, 64, stride=BLOCKS), :] for half in range(2)], axis=1)
-        pair = pair.astype(bf16)
-        snap_b[i] = pair
-        return total + lax.dot_general(pair, pair, (((1,), (1,)), ((), ())), preferred_element_type=f32)
-
-    local = lax.fori_loop(0, BLOCKS // 2, gram_step, jnp.zeros((64, 64), f32))
-    local = jnp.concatenate([local, jnp.zeros((64, 64), f32)], axis=1)
-    for b in range(8):
-        gram[b] = local[8 * b : 8 * b + 8]
-
-    def exchange(sources, target, me, count, device_of, send, recv, first):
-        copies = []
-        for d in range(1, count):
-            peer = lax.rem(me + d, count)
-            copies.append(
-                remote(sources(peer), target.at[me], send.at[first + d], recv.at[first + d], device_of(peer))
-            )
-        for copy in copies:
-            copy.start()
-        return copies
-
-    def total(ref, count):
-        value = ref[0]
-        for i in range(1, count):
-            value = value + ref[i]
-        return value
-
-    copies = exchange(lambda peer: gram.at[peer], gram_part, gy, n_gy, on_gy, gram_send, gram_recv, 0)
-    gram_part[gy] = gram[gy]
-
-    def loop(start, stop, step):
-        lax.fori_loop(start, stop, lambda x, _: (step(x), 0)[1], 0)
+    start(corner_copies)
+    if FAR_AT == 0:
+        start(far_copies)
 
     loop(2, 2 + X, lambda x: primitive_layer(state, prim, x))
-    for copy in copies:
-        copy.wait()
+    wait(scatter)
     gram_sums[0] = total(gram_part, n_gy)
     copies = exchange(lambda peer: gram_sums.at[0], gram_z, iz, n_z, on_z, gram_send, gram_recv, 8)
     gram_z[iz] = gram_sums[0]
-    for copy in y_copies:
-        copy.wait()
+    if FAR_AT == 1:
+        start(far_copies)
+    wait(y_copies)
     for side in range(2):
         place_rows(state, prim, y_in, side)
     loop(3, 1 + X, lambda x: first_layer(state, prim, state2, prim2, x))
-    for copy in copies:
-        copy.wait()
+    sums[...] = jnp.zeros_like(sums)
+    wait(copies)
     gram_sums[1] = total(gram_z, n_z)
     copies = exchange(lambda peer: gram_sums.at[1], gram_y, iy, n_y, on_y, gram_send, gram_recv, 16)
     gram_y[iy] = gram_sums[1]
-    for copy in far_copies:
-        copy.start()
-    for copy in copies:
-        copy.wait()
-    gram_sums[2] = total(gram_y, n_y)
-    copies = exchange(lambda peer: gram_sums.at[2], gram_all, gy, n_gy, on_gy, gram_send, gram_recv, 24)
-    gram_all[gy] = gram_sums[2]
-
-    sums[...] = jnp.zeros_like(sums)
-    for copy in near_copies + corner_copies:
-        copy.wait()
+    if FAR_AT == 2:
+        start(far_copies)
+    wait(near_copies + corner_copies)
     loop(0, 2, lambda i: primitive_layer(state, prim, 1 + 9 * i))
     for side_x in range(2):
         for side_y in range(2):
@@ -398,9 +415,65 @@
     loop(0, 2, lambda i: first_layer(state, prim, state2, prim2, 2 + 7 * i))
     for side in range(2):
         edge_rows(state, prim, state2, prim2, y_in, side)
-    for copy in copies:
-        copy.wait()
-
+    wait(copies)
+    gram_sums[2] = total(gram_y, n_y)
+    gather = exchange(lambda peer: gram_sums.at[2], gram_all, gy, n_gy, on_gy, gram_send, gram_recv, 24)
+    gram_all[gy] = gram_sums[2]
+    loop(3, 1 + X, lambda x: second_layer(state, state2, prim2, updated, sums, x))
+    wait(far_copies)
+    loop(0, 2, lambda i: primitive_layer(state, prim, 11 * i))
+    loop(0, 2, lambda i: first_layer(state, prim, state2, prim2, 1 + 9 * i))
+    loop(0, 2, lambda i: second_layer(state, state2, prim2, updated, sums, 2 + 7 * i))
+
+    flat_sums = flat(sums)
+    columns = []
+    for half in range(2):
+        for t in range(2):
+            parts = []
+            for c in range(6):
+                begin = (c * 2 + t) * Y + 4 * half
+                part = flat_sums[pl.ds(begin, 8, stride=8), :]
+                for k in range(1, 4):
+                    part = part + flat_sums[pl.ds(begin + k, 8, stride=8), :]
+                parts.append(part)
+            columns.append(jnp.concatenate(parts, axis=0))
+    fine = jnp.concatenate(columns, axis=1)
+    source = lax.broadcasted_iota(jnp.int32, (512, 128), 0)
+    target = lax.broadcasted_iota(jnp.int32, (512, 128), 1)
+    selection = jnp.where(lax.shift_right_logical(source, 2) == target, 1.0 / 64.0, 0.0).astype(bf16)
+    means = sum(jnp.dot(part, selection, preferred_element_type=f32) for part in split3(fine))
+    for c in range(3):
+        for half in range(2):
+            at = (2 * c + half) * 8
+            coarse[pl.ds(16 * c + half, 8, stride=2), :] = means[at : at + 8]
+
+    def dot_step(i, acc):
+        for part in range(4):
+            b = 4 * i + part
+            acc = acc + flat_snap[pl.ds(b, 64, stride=BLOCKS), :] * coarse[pl.ds(b, 1), :]
+        return acc
+
+    acc = lax.fori_loop(0, BLOCKS // 4, dot_step, jnp.zeros((64, 128), f32))
+    squares = jnp.sum(coarse[...] * coarse[...], axis=0, keepdims=True)
+    acc = jnp.where(lax.broadcasted_iota(jnp.int32, (64, 128), 0) == SNAPS, squares, acc)
+    ones = jnp.ones((8, 128), bf16)
+    products = sum(
+        lax.dot_general(ones, part, (((1,), (1,)), ((), ())), preferred_element_type=f32) for part in split3(acc)
+    )
+    dot_sums[0] = jnp.concatenate([products, jnp.zeros((8, 64), f32)], axis=1)
+    copies = exchange(lambda peer: dot_sums.at[0], dot_gy, gy, n_gy, on_gy, dot_send, dot_recv, 0)
+    dot_gy[gy] = dot_sums[0]
+
+    stores = []
+    for t in range(2):
+        lanes = pl.ds(128 * t, 128)
+        stores += [
+            pltpu.make_async_copy(updated.at[0, :, t], out_density.at[:, :, lanes], store_sem.at[3 * t]),
+            pltpu.make_async_copy(updated.at[pl.ds(1, 3), :, t], out_momentum.at[:, :, :, lanes], store_sem.at[3 * t + 1]),
+            pltpu.make_async_copy(updated.at[4, :, t], out_energy.at[:, :, lanes], store_sem.at[3 * t + 2]),
+        ]
+    start(stores)
+    wait(gather)
     lane = lax.broadcasted_iota(jnp.int32, (8, 128), 1)
     sub = lax.broadcasted_iota(jnp.int32, (8, 128), 0)
     blocks = []
@@ -409,106 +482,59 @@
         known = (row < SNAPS) & (lane < SNAPS)
         unit = ((lane == row) & (row == SNAPS)) | (lane == row + 64)
         blocks.append(jnp.where(known, gram_all[b] / rows_all, jnp.where(unit, 1.0, 0.0)))
-    blocks = eliminate(blocks)
-    lower = []
+    blocks = eliminate(blocks, 0, SPLIT)
+    wait(copies)
+    dot_sums[1] = total(dot_gy, n_gy)
+    copies = exchange(lambda peer: dot_sums.at[1], dot_z, iz, n_z, on_z, dot_send, dot_recv, 8)
+    dot_z[iz] = dot_sums[1]
+    blocks = eliminate(blocks, SPLIT, SNAPS - 1)
     for b in range(8):
         row = sub + 8 * b
         diagonal = jnp.sum(jnp.where(lane == row, blocks[b], 0.0), axis=1, keepdims=True)
         scaled = blocks[b] * (1.0 / jnp.sqrt(diagonal))
         factor_v[b] = jnp.where((lane >= row) & (lane < SNAPS), scaled, 0.0)
-        lower.append(jnp.where(row < SNAPS, pltpu.roll(scaled, 64, 1), 0.0))
-    lower = jnp.concatenate(lower, axis=0)[:, :64]
-    stacked = jnp.concatenate(split3(lower), axis=0)
+        lower_v[b] = jnp.where((row < SNAPS) & (lane < 64), pltpu.roll(scaled, 64, 1), 0.0)
+    wait(copies)
+    dot_sums[2] = total(dot_z, n_z)
+    copies = exchange(lambda peer: dot_sums.at[2], dot_y, iy, n_y, on_y, dot_send, dot_recv, 16)
+    dot_y[iy] = dot_sums[2]
+    stacked = jnp.concatenate(split3(lower_v[...].reshape(64, 128)[:, :64]), axis=0)
 
     def modes_step(i, carry):
-        parts = jnp.dot(stacked, snap_b[i], preferred_element_type=f32)
-        both = parts[0:64] + (parts[64:128] + parts[128:192])
-        for half in range(2):
-            flat_modes[pl.ds(2 * i + half, 64, stride=BLOCKS), :] = both[:, 128 * half : 128 * half + 128]
+        for part in range(UNROLL):
+            at = UNROLL * i + part
+            parts = jnp.dot(stacked, snap_b[at], preferred_element_type=f32)
+            both = parts[0:64] + (parts[64:128] + parts[128:192])
+            for half in range(2):
+                flat_modes[pl.ds(2 * at + half, 64, stride=BLOCKS), :] = both[:, 128 * half : 128 * half + 128]
         return carry
 
-    lax.fori_loop(0, BLOCKS // 2, modes_step, 0)
+    lax.fori_loop(0, BLOCKS // 2 // UNROLL, modes_step, 0)
     store_modes = pltpu.make_async_copy(
         flat_modes.at[pl.ds(0, SNAPS * BLOCKS)], out_modes.at[pl.ds(0, SNAPS * BLOCKS)], store_sem.at[6]
     )
     store_modes.start()
-
-    loop(4, X, lambda x: second_layer(state, state2, prim2, updated, sums, x))
-    for copy in far_copies:
-        copy.wait()
-    loop(0, 2, lambda i: primitive_layer(state, prim, 11 * i))
-    loop(0, 2, lambda i: first_layer(state, prim, state2, prim2, 1 + 9 * i))
-    loop(2, 4, lambda x: second_layer(state, state2, prim2, updated, sums, x))
-    loop(X, 2 + X, lambda x: second_layer(state, state2, prim2, updated, sums, x))
-    stores = [store_modes]
-    for t in range(2):
-        lanes = pl.ds(128 * t, 128)
-        stores += [
-            pltpu.make_async_copy(updated.at[0, :, t], out_density.at[:, :, lanes], store_sem.at[3 * t]),
-            pltpu.make_async_copy(updated.at[pl.ds(1, 3), :, t], out_momentum.at[:, :, :, lanes], store_sem.at[3 * t + 1]),
-            pltpu.make_async_copy(updated.at[4, :, t], out_energy.at[:, :, lanes], store_sem.at[3 * t + 2]),
-        ]
-    for copy in stores[1:]:
-        copy.start()
-
-    flat_sums = flat(sums)
-    columns = []
-    for half in range(2):
-        for t in range(2):
-            parts = []
-            for c in range(6):
-                start = (c * 2 + t) * Y + 4 * half
-                part = flat_sums[pl.ds(start, 8, stride=8), :]
-                for k in range(1, 4):
-                    part = part + flat_sums[pl.ds(start + k, 8, stride=8), :]
-                parts.append(part)
-            columns.append(jnp.concatenate(parts, axis=0))
-    fine = jnp.concatenate(columns, axis=1)
-    source = lax.broadcasted_iota(jnp.int32, (512, 128), 0)
-    target = lax.broadcasted_iota(jnp.int32, (512, 128), 1)
-    gather = jnp.where(lax.shift_right_logical(source, 2) == target, 1.0 / 64.0, 0.0).astype(bf16)
-    means = sum(jnp.dot(part, gather, preferred_element_type=f32) for part in split3(fine))
-    for c in range(3):
-        for half in range(2):
-            first = (2 * c + half) * 8
-            coarse[pl.ds(16 * c + half, 8, stride=2), :] = means[first : first + 8]
-
-    def dot_step(i, acc):
-        for part in range(4):
-            b = 4 * i + part
-            acc = acc + flat_modes[pl.ds(b, 64, stride=BLOCKS), :] * coarse[pl.ds(b, 1), :]
-        return acc
-
-    acc = lax.fori_loop(0, BLOCKS // 4, dot_step, jnp.zeros((64, 128), f32))
-    squares = jnp.sum(coarse[...] * coarse[...], axis=0, keepdims=True)
-    acc = jnp.where(lax.broadcasted_iota(jnp.int32, (64, 128), 0) == SNAPS, squares, acc)
-    ones = jnp.ones((8, 128), bf16)
-    products = sum(
-        lax.dot_general(ones, part, (((1,), (1,)), ((), ())), preferred_element_type=f32) for part in split3(acc)
-    )
-    dot_sums[0] = jnp.concatenate([products, jnp.zeros((8, 64), f32)], axis=1)
-    stages = ((dot_gy, gy, n_gy, on_gy, 0), (dot_z, iz, n_z, on_z, 8), (dot_y, iy, n_y, on_y, 16))
-    for stage, (target, me, count, device_of, first) in enumerate(stages):
-        copies = exchange(lambda peer: dot_sums.at[stage], target, me, count, device_of, dot_send, dot_recv, first)
-        target[me] = dot_sums[stage]
-        for copy in copies:
-            copy.wait()
-        dot_sums[stage + 1] = total(target, count)
-    share = dot_sums[3] / rows_all
-
-    rest = jnp.where(lane < SNAPS, share, 0.0)
-    norm = jnp.sum(jnp.where(lane == SNAPS, share, 0.0), axis=1, keepdims=True)
-    last = jnp.sqrt(norm - jnp.sum(rest * rest, axis=1, keepdims=True))
+    wait(copies)
+    share = total(dot_y, n_y) / rows_all
+
+    own = jnp.where(lane < SNAPS, share, 0.0)
+    left = jnp.sum(jnp.where(lane == SNAPS, share, 0.0), axis=1, keepdims=True)[0:1]
+    weights = []
+    for b in range(8):
+        weights.append(jnp.sum(lower_v[b] * own, axis=1, keepdims=True))
+        left = left - jnp.sum(weights[b] * weights[b], axis=0, keepdims=True)
+    last = jnp.broadcast_to(jnp.sqrt(left), (8, 128))
+    mode = [coarse[8 * i : 8 * i + 8, :] for i in range(6)]
     for b in range(8):
         row = sub + 8 * b
-        column = jnp.sum(jnp.where(lane == row, rest, 0.0), axis=1, keepdims=True)
-        column = jnp.where(row == SNAPS, last, column)
+        weight = jnp.broadcast_to(weights[b], (8, 128))
+        column = jnp.where(row == SNAPS, last, weight)
         out_factor[8 * b : 8 * b + 8, :] = jnp.where(lane == SNAPS, column, factor_v[b])[:, :64]
-    mode = [coarse[8 * i : 8 * i + 8, :] for i in range(6)]
-    for m in range(SNAPS):
-        weight = jnp.broadcast_to(rest[:, m : m + 1], (8, 128))
-        for i in range(6):
-            mode[i] = mode[i] - weight * flat_modes[BLOCKS * m + 8 * i : BLOCKS * m + 8 * i + 8, :]
+        for at in range(8 if b < 7 else 7):
+            one = jnp.broadcast_to(weight[at : at + 1], (8, 128))
+            begin = BLOCKS * (8 * b + at)
+            for i in range(6):
+                mode[i] = mode[i] - one * flat_modes[begin + 8 * i : begin + 8 * i + 8, :]
     scale = 1.0 / last
     for i in range(6):
         flat_modes[BLOCKS * SNAPS + 8 * i : BLOCKS * SNAPS + 8 * i + 8, :] = mode[i] * scale
@@ -516,7 +542,20 @@
         flat_modes.at[pl.ds(SNAPS * BLOCKS, BLOCKS)], out_modes.at[pl.ds(SNAPS * BLOCKS, BLOCKS)], store_sem.at[7]
     )
     store_last.start()
-    for copy in stores + [store_last]:
+    wait(stores + [store_modes, store_last])
+
+
+def copy_out(*refs):
+    sources, targets, sem = refs[:5], refs[5:10], refs[10]
+    copies = []
+    for i, (source, target) in enumerate(zip(sources, targets)):
+        if source.ndim == 4:
+            copies += [pltpu.make_async_copy(source.at[c], target.at[c], sem.at[5 + c]) for c in range(3)]
+        else:
+            copies.append(pltpu.make_async_copy(source, target, sem.at[i]))
+    for copy in copies:
+        copy.start()
+    for copy in copies:
         copy.wait()
 
 
@@ -531,10 +570,10 @@
         anywhere = pl.BlockSpec(memory_space=pl.ANY)
         vmem = pl.BlockSpec(memory_space=pltpu.VMEM)
         dma = pltpu.SemaphoreType.DMA
-        new_density, new_momentum, new_energy, factor, modes = pl.pallas_call(
+        results = pl.pallas_call(
             functools.partial(kernel, float(rows_all), (n_gx, n_gy, n_y)),
             name="sections_and_modes",
-            in_specs=[anywhere] * 4,
+            in_specs=[pl.BlockSpec(memory_space=pltpu.HBM)] * 4,
             out_specs=(anywhere, anywhere, anywhere, vmem, anywhere),
             out_shape=(
                 jax.ShapeDtypeStruct((X, Y, Z), f32),
@@ -558,6 +597,7 @@
                 pltpu.VMEM((64, 3, 16, 128), f32),
                 pltpu.VMEM((BLOCKS // 2, 64, 256), bf16),
                 pltpu.VMEM((64, 3, 16, 128), f32),
+                pltpu.VMEM((8, 8, 128), f32),
                 pltpu.VMEM((8, 8, 128), f32),
                 pltpu.VMEM((BLOCKS, 128), f32),
                 pltpu.VMEM((8, 8, 128), f32),
@@ -586,7 +626,16 @@
             compiler_params=pltpu.CompilerParams(
                 collective_id=0, has_side_effects=True, vmem_limit_bytes=32 * 2**20
             ),
-        )(density, momentum, energy, snapshots)
+        )(*(pltpu.with_memory_space_constraint(a, pltpu.HBM) for a in (density, momentum, energy, snapshots)))
+        new_density, new_momentum, new_energy, factor, modes = pl.pallas_call(
+            copy_out,
+            name="copy_out",
+            in_specs=[anywhere] * 5,
+            out_specs=[pl.BlockSpec(memory_space=pltpu.HBM)] * 5,
+            out_shape=[jax.ShapeDtypeStruct(value.shape, f32) for value in results],
+            scratch_shapes=[dma((8,))],
+            compiler_params=pltpu.CompilerParams(vmem_limit_bytes=2**20),
+        )(*results)
         modes = modes.reshape(64, 3, 8, 2, 128).transpose(0, 1, 3, 2, 4).reshape(64, 3, 2, 1024)
         return new_density, new_momentum, new_energy, factor, modes
 

time: 68.8 us -> 53.6 us (0.78)
  local copies, waits for them, and re-layouts: 9.1 us -> 0 us
  Pallas kernels: 58.8 us -> 52.9 us
    unnamed x13 -> x0, local copies, waits for them, and re-layouts: 9.1 us -> none
    pallas_call x1, Pallas kernels: 58.8 us -> 50.8 us  [on_device(): pl.pallas_call(functools.partial(kernel, float(rows_all), (n_gx, n_gy, n_...]
    pallas_call x0 -> x1, Pallas kernels: none -> 2.09 us  [on_device(): pl.pallas_call(copy_out, name='copy_out', in_specs=[anywhere] * 5, out_sp...]
where the time goes in v2:
time: 53.6 us; the launch traced here: 53.5 us
  Pallas kernels  52.9 us (99%)
  between operations  0.64 us (1%)
    pallas_call x1, Pallas kernels, on_device(): pl.pallas_call(functools.partial(kernel, float(rows_all), (n_gx, n_gy, n_...  50.8 us
    pallas_call x1, Pallas kernels, on_device(): pl.pallas_call(copy_out, name='copy_out', in_specs=[anywhere] * 5, out_sp...  2.09 us

profile of v2, /device:TPU:1, one launch (start us, length us, event | category | flops | bytes accessed | tf_op | source)
XLA Modules:
  0.0 53.5 jit_solution(10200273222785511367)
XLA Ops:
  0.6 50.8 %sections_and_modes.1 = (f32[8,64,256]{2,1,0:T(8,128)S(1)}, f32[3,8,64,256]{3,2,1,0:T(8,128)S(1)}, f32[8,64,256]{2,1,0:T(8,128)S(1)}, f32[64,64]{1,0:T(8,128)S(1)}, f32[3072,128]{1,0:T(8,128)S(1)}) custom-call(f32[8,64,256]{2,1,0:T(8,128)} %density.1, f32[3,8,64,256]{3,2,1,0:T(8,128)} %momentum.1, f32[8,64,256]{2,1,0:T(8,128)} %energy.1, ...), custom_call_target="tpu_custom_call" | custom-call | tf_op jit(solution)/shard_map/sections_and_modes/pallas_call | solution.py:573
  51.4 2.1 %copy_out.1 = (f32[8,64,256]{2,1,0:T(8,128)}, f32[3,8,64,256]{3,2,1,0:T(8,128)}, f32[8,64,256]{2,1,0:T(8,128)}, f32[64,64]{1,0:T(8,128)}, f32[3072,128]{1,0:T(8,128)}) custom-call(f32[8,64,256]{2,1,0:T(8,128)S(1)} %get-tuple-element.15.refs_0_, f32[3,8,64,256]{3,2,1,0:T(8,128)S(1)} %get-tuple-element.16.refs_1_, ...), custom_call_target="tpu_custom_call" | custom-call | tf_op jit(solution)/shard_map/copy_out/pallas_call | solution.py:630

commit v3 on v2

--- a/solution.py
+++ b/solution.py
@@ -21,9 +21,12 @@
 SNAPS = 63
 BLOCKS = 48
 CHUNK = 32
-UNROLL = 4
-FAR_AT = 0
-SPLIT = 24
+UNROLL = 8
+FAR_LOW = 1
+FAR_HIGH = 2
+Y_FIRST = True
+FACTOR_AT = 1
+SPLIT = 4
 
 
 def flat(ref):
@@ -194,31 +197,28 @@
 
 def eliminate(rows, first, stop):
     sub = lax.broadcasted_iota(jnp.int32, (8, 128), 0)
-
-    def along_lanes(value, k):
-        return jnp.broadcast_to(value[:, k : k + 1], (8, 128))
-
-    def along_rows(value, k):
-        return jnp.broadcast_to(value[k : k + 1, :], (8, 128))
-
-    for k in range(first, stop, 2):
-        block, at = divmod(k, 8)
-        left = {b: along_lanes(rows[b], k) for b in range(block, 8)}
-        right = {b: along_lanes(rows[b], k + 1) for b in range(block, 8)}
-        cross = along_rows(left[block], at + 1)
-        inverse = 1.0 / along_rows(left[block], at)
-        ratio = cross * inverse
-        pivot = along_rows(right[block], at + 1) - ratio * cross
-        row = along_rows(rows[block], at)
-        next_row = along_rows(rows[block], at + 1) - ratio * row
-        row = row * inverse
-        next_row = next_row * (1.0 / pivot)
-        for b in range(block, 8):
-            first_column, second_column = left[b], right[b] - ratio * left[b]
-            if b == block:
-                first_column = jnp.where(sub > at, first_column, 0.0)
-                second_column = jnp.where(sub > at + 1, second_column, 0.0)
-            rows[b] = rows[b] - first_column * row - second_column * next_row
+    for block in range(first, stop):
+        columns = [
+            [jnp.broadcast_to(rows[b][:, 8 * block + j : 8 * block + j + 1], (8, 128)) for b in range(block, 8)]
+            for j in range(8)
+        ]
+        corner = {
+            (i, j): jnp.broadcast_to(columns[j][0][i : i + 1, :], (8, 128)) for j in range(8) for i in range(j, 8)
+        }
+        pivot_rows = [jnp.broadcast_to(rows[block][i : i + 1, :], (8, 128)) for i in range(8)]
+        for j in range(8):
+            inverse = 1.0 / corner[j, j]
+            ratio = {i: corner[i, j] * inverse for i in range(j + 1, 8)}
+            for i in range(j + 1, 8):
+                for n in range(j + 1, i + 1):
+                    corner[i, n] = corner[i, n] - ratio[i] * corner[n, j]
+                pivot_rows[i] = pivot_rows[i] - ratio[i] * pivot_rows[j]
+                for b in range(8 - block):
+                    columns[i][b] = columns[i][b] - ratio[i] * columns[j][b]
+            scaled = pivot_rows[j] * inverse
+            for b in range(8 - block):
+                column = jnp.where(sub > j, columns[j][b], 0.0) if b == 0 else columns[j][b]
+                rows[block + b] = rows[block + b] - column * scaled
     return rows
 
 
@@ -333,6 +333,22 @@
         return value
 
     near_copies, far_copies = x_copies(0), x_copies(1)
+
+    def start_far(point):
+        for t, chosen in enumerate((FAR_LOW, FAR_HIGH)):
+            if chosen == point:
+                start(far_copies[3 * t : 3 * t + 3] + far_copies[6 + 3 * t : 9 + 3 * t])
+
+    along_z, along_y = (gram_z, iz, n_z, on_z), (gram_y, iy, n_y, on_y)
+    second, third = (along_y, along_z) if Y_FIRST else (along_z, along_y)
+
+    def gram_stage(stage, value):
+        target, me, count, device_of = (second, third)[stage]
+        gram_sums[stage] = value
+        copies = exchange(lambda peer: gram_sums.at[stage], target, me, count, device_of, gram_send, gram_recv, 8 + 8 * stage)
+        target[me] = value
+        return copies
+
     start(near_copies)
 
     load_snapshots.wait()
@@ -386,27 +402,20 @@
                 )
             )
     start(corner_copies)
-    if FAR_AT == 0:
-        start(far_copies)
+    start_far(0)
 
     loop(2, 2 + X, lambda x: primitive_layer(state, prim, x))
     wait(scatter)
-    gram_sums[0] = total(gram_part, n_gy)
-    copies = exchange(lambda peer: gram_sums.at[0], gram_z, iz, n_z, on_z, gram_send, gram_recv, 8)
-    gram_z[iz] = gram_sums[0]
-    if FAR_AT == 1:
-        start(far_copies)
+    copies = gram_stage(0, total(gram_part, n_gy))
+    start_far(1)
     wait(y_copies)
     for side in range(2):
         place_rows(state, prim, y_in, side)
     loop(3, 1 + X, lambda x: first_layer(state, prim, state2, prim2, x))
     sums[...] = jnp.zeros_like(sums)
     wait(copies)
-    gram_sums[1] = total(gram_z, n_z)
-    copies = exchange(lambda peer: gram_sums.at[1], gram_y, iy, n_y, on_y, gram_send, gram_recv, 16)
-    gram_y[iy] = gram_sums[1]
-    if FAR_AT == 2:
-        start(far_copies)
+    copies = gram_stage(1, total(second[0], second[2]))
+    start_far(2)
     wait(near_copies + corner_copies)
     loop(0, 2, lambda i: primitive_layer(state, prim, 1 + 9 * i))
     for side_x in range(2):
@@ -416,10 +425,25 @@
     for side in range(2):
         edge_rows(state, prim, state2, prim2, y_in, side)
     wait(copies)
-    gram_sums[2] = total(gram_y, n_y)
+    gram_sums[2] = total(third[0], third[2])
     gather = exchange(lambda peer: gram_sums.at[2], gram_all, gy, n_gy, on_gy, gram_send, gram_recv, 24)
     gram_all[gy] = gram_sums[2]
     loop(3, 1 + X, lambda x: second_layer(state, state2, prim2, updated, sums, x))
+    lane = lax.broadcasted_iota(jnp.int32, (8, 128), 1)
+    sub = lax.broadcasted_iota(jnp.int32, (8, 128), 0)
+
+    def factor_start():
+        wait(gather)
+        blocks = []
+        for b in range(8):
+            row = sub + 8 * b
+            known = (row < SNAPS) & (lane < SNAPS)
+            unit = ((lane == row) & (row == SNAPS)) | (lane == row + 64)
+            blocks.append(jnp.where(known, gram_all[b] / rows_all, jnp.where(unit, 1.0, 0.0)))
+        return eliminate(blocks, 0, SPLIT)
+
+    if FACTOR_AT == 2:
+        blocks = factor_start()
     wait(far_copies)
     loop(0, 2, lambda i: primitive_layer(state, prim, 11 * i))
     loop(0, 2, lambda i: first_layer(state, prim, state2, prim2, 1 + 9 * i))
@@ -473,21 +497,15 @@
             pltpu.make_async_copy(updated.at[4, :, t], out_energy.at[:, :, lanes], store_sem.at[3 * t + 2]),
         ]
     start(stores)
-    wait(gather)
-    lane = lax.broadcasted_iota(jnp.int32, (8, 128), 1)
-    sub = lax.broadcasted_iota(jnp.int32, (8, 128), 0)
-    blocks = []
-    for b in range(8):
-        row = sub + 8 * b
-        known = (row < SNAPS) & (lane < SNAPS)
-        unit = ((lane == row) & (row == SNAPS)) | (lane == row + 64)
-        blocks.append(jnp.where(known, gram_all[b] / rows_all, jnp.where(unit, 1.0, 0.0)))
-    blocks = eliminate(blocks, 0, SPLIT)
+    if FACTOR_AT == 0:
+        blocks = factor_start()
     wait(copies)
     dot_sums[1] = total(dot_gy, n_gy)
     copies = exchange(lambda peer: dot_sums.at[1], dot_z, iz, n_z, on_z, dot_send, dot_recv, 8)
     dot_z[iz] = dot_sums[1]
-    blocks = eliminate(blocks, SPLIT, SNAPS - 1)
+    if FACTOR_AT == 1:
+        blocks = factor_start()
+    blocks = eliminate(blocks, SPLIT, 8)
     for b in range(8):
         row = sub + 8 * b
         diagonal = jnp.sum(jnp.where(lane == row, blocks[b], 0.0), axis=1, keepdims=True)
@@ -501,15 +519,15 @@
     stacked = jnp.concatenate(split3(lower_v[...].reshape(64, 128)[:, :64]), axis=0)
 
     def modes_step(i, carry):
-        for part in range(UNROLL):
-            at = UNROLL * i + part
+        for part in range(BLOCKS // 2):
+            at = BLOCKS // 2 * i + part
             parts = jnp.dot(stacked, snap_b[at], preferred_element_type=f32)
             both = parts[0:64] + (parts[64:128] + parts[128:192])
             for half in range(2):
                 flat_modes[pl.ds(2 * at + half, 64, stride=BLOCKS), :] = both[:, 128 * half : 128 * half + 128]
         return carry
 
-    lax.fori_loop(0, BLOCKS // 2 // UNROLL, modes_step, 0)
+    lax.fori_loop(0, 1, modes_step, 0)
     store_modes = pltpu.make_async_copy(
         flat_modes.at[pl.ds(0, SNAPS * BLOCKS)], out_modes.at[pl.ds(0, SNAPS * BLOCKS)], store_sem.at[6]
     )
@@ -548,11 +566,24 @@
 def copy_out(*refs):
     sources, targets, sem = refs[:5], refs[5:10], refs[10]
     copies = []
-    for i, (source, target) in enumerate(zip(sources, targets)):
+
+    def add(source, target):
+        copies.append(pltpu.make_async_copy(source, target, sem.at[len(copies)]))
+
+    for source, target in zip(sources, targets):
         if source.ndim == 4:
-            copies += [pltpu.make_async_copy(source.at[c], target.at[c], sem.at[5 + c]) for c in range(3)]
+            for c in range(source.shape[0]):
+                for half in range(2):
+                    part = pl.ds(source.shape[1] // 2 * half, source.shape[1] // 2)
+                    add(source.at[c, part], target.at[c, part])
+        elif source.shape[0] == 64:
+            add(source, target)
         else:
-            copies.append(pltpu.make_async_copy(source, target, sem.at[i]))
+            pieces = 2 if source.ndim == 3 else 6
+            size = source.shape[0] // pieces
+            for piece in range(pieces):
+                part = pl.ds(size * piece, size)
+                add(source.at[part], target.at[part])
     for copy in copies:
         copy.start()
     for copy in copies:
@@ -633,7 +664,7 @@
             in_specs=[anywhere] * 5,
             out_specs=[pl.BlockSpec(memory_space=pltpu.HBM)] * 5,
             out_shape=[jax.ShapeDtypeStruct(value.shape, f32) for value in results],
-            scratch_shapes=[dma((8,))],
+            scratch_shapes=[dma((17,))],
             compiler_params=pltpu.CompilerParams(vmem_limit_bytes=2**20),
         )(*results)
         modes = modes.reshape(64, 3, 8, 2, 128).transpose(0, 1, 3, 2, 4).reshape(64, 3, 2, 1024)

time: 53.6 us -> 45.8 us (0.85)
  Pallas kernels: 52.9 us -> 45.1 us
    pallas_call x1, Pallas kernels: 50.8 us -> 43 us  [on_device(): pl.pallas_call(functools.partial(kernel, float(rows_all), (n_gx, n_gy, n_...]
where the time goes in v3:
time: 45.8 us
  Pallas kernels  45.1 us (98%)
  between operations  0.64 us (1%)
    pallas_call x1, Pallas kernels, on_device(): pl.pallas_call(functools.partial(kernel, float(rows_all), (n_gx, n_gy, n_...  43 us
    pallas_call x1, Pallas kernels, on_device(): pl.pallas_call(copy_out, name='copy_out', in_specs=[anywhere] * 5, out_sp...  2.16 us

profile of v3, /device:TPU:1, one launch (start us, length us, event | category | flops | bytes accessed | tf_op | source)
XLA Modules:
  0.0 45.8 jit_solution(9592376913976500217)
XLA Ops:
  0.6 43.0 %sections_and_modes.1 = (f32[8,64,256]{2,1,0:T(8,128)S(1)}, f32[3,8,64,256]{3,2,1,0:T(8,128)S(1)}, f32[8,64,256]{2,1,0:T(8,128)S(1)}, f32[64,64]{1,0:T(8,128)S(1)}, f32[3072,128]{1,0:T(8,128)S(1)}) custom-call(f32[8,64,256]{2,1,0:T(8,128)} %density.1, f32[3,8,64,256]{3,2,1,0:T(8,128)} %momentum.1, f32[8,64,256]{2,1,0:T(8,128)} %energy.1, ...), custom_call_target="tpu_custom_call" | custom-call | tf_op jit(solution)/shard_map/sections_and_modes/pallas_call | solution.py:604
  43.6 2.2 %copy_out.1 = (f32[8,64,256]{2,1,0:T(8,128)}, f32[3,8,64,256]{3,2,1,0:T(8,128)}, f32[8,64,256]{2,1,0:T(8,128)}, f32[64,64]{1,0:T(8,128)}, f32[3072,128]{1,0:T(8,128)}) custom-call(f32[8,64,256]{2,1,0:T(8,128)S(1)} %get-tuple-element.15.refs_0_, f32[3,8,64,256]{3,2,1,0:T(8,128)S(1)} %get-tuple-element.16.refs_1_, ...), custom_call_target="tpu_custom_call" | custom-call | tf_op jit(solution)/shard_map/copy_out/pallas_call | solution.py:661

commit v4 on v3

--- a/solution.py
+++ b/solution.py
@@ -100,16 +100,16 @@
     )
 
 
-def primitive_layer(state, prim, x):
-    for row in range(8, 8 + Y, CHUNK):
+def primitive_layer(state, prim, x, begin=0, end=Y):
+    for row in range(8 + begin, 8 + end, CHUNK):
         for t in range(2):
             values = primitives([state[f, x, t, pl.ds(row, CHUNK), :] for f in range(5)])
             for f in range(4):
                 prim[f, x, t, pl.ds(row, CHUNK), :] = values[f]
 
 
-def first_layer(state, prim, state2, prim2, x):
-    for row in range(8, 8 + Y, CHUNK):
+def first_layer(state, prim, state2, prim2, x, begin=0, end=Y):
+    for row in range(8 + begin, 8 + end, CHUNK):
         delta = change_rows(prim, state, x, row, CHUNK)
         for t in range(2):
             new = [state[f, x, t, pl.ds(row, CHUNK), :] + delta[f][t] for f in range(5)]
@@ -120,8 +120,8 @@
                 prim2[f, x, t, pl.ds(row, CHUNK), :] = values[f]
 
 
-def second_layer(state, state2, prim2, updated, sums, x):
-    for row in range(8, 8 + Y, CHUNK):
+def second_layer(state, state2, prim2, updated, sums, x, begin=0, end=Y):
+    for row in range(8 + begin, 8 + end, CHUNK):
         delta = change_rows(prim2, state2, x, row, CHUNK)
         for t in range(2):
             new = [
@@ -225,7 +225,7 @@
 def kernel(
     rows_all, sizes,
     density, momentum, energy, snapshots,
-    out_density, out_momentum, out_energy, out_factor, out_modes,
+    out_density, out_momentum, out_energy, out_factor, out_modes, out_last,
     state, prim, state2, prim2, updated, sums,
     y_out, y_in, corner_out, corner_in,
     snap_in, snap_f, snap_b, modes, factor_v, lower_v, coarse,
@@ -281,28 +281,29 @@
             src_ref=source, dst_ref=target, send_sem=send_sem, recv_sem=recv_sem, device_id=device, device_id_type=MESH
         )
 
-    def x_copies(layer):
+    def x_copies(layer, begin, count, at):
         copies = []
         for side in range(2):
             source, target = (X - 1 - layer, 1 - layer) if side == 0 else (layer, 10 + layer)
             device = moved(1, 0) if side == 0 else moved(-1, 0)
+            own, rows = pl.ds(begin, count), pl.ds(8 + begin, count)
             for t in range(2):
-                lanes, rows = pl.ds(128 * t, 128), pl.ds(8, Y)
-                at = ((layer * 2 + side) * 2 + t) * 3
+                lanes = pl.ds(128 * t, 128)
                 copies += [
                     remote(
-                        density.at[source, :, lanes], state.at[0, target, t, rows, :],
+                        density.at[source, own, lanes], state.at[0, target, t, rows, :],
                         x_send.at[at], x_recv.at[at], device,
                     ),
                     remote(
-                        momentum.at[:, source, :, lanes], state.at[pl.ds(1, 3), target, t, rows, :],
+                        momentum.at[:, source, own, lanes], state.at[pl.ds(1, 3), target, t, rows, :],
                         x_send.at[at + 1], x_recv.at[at + 1], device,
                     ),
                     remote(
-                        energy.at[source, :, lanes], state.at[4, target, t, rows, :],
+                        energy.at[source, own, lanes], state.at[4, target, t, rows, :],
                         x_send.at[at + 2], x_recv.at[at + 2], device,
                     ),
                 ]
+                at += 3
         return copies
 
     def start(copies):
@@ -332,12 +333,13 @@
             value = value + ref[i]
         return value
 
-    near_copies, far_copies = x_copies(0), x_copies(1)
+    near_copies = x_copies(0, 0, Y, 0)
+    far_copies = [x_copies(1, CHUNK * half, CHUNK, 12 + 12 * half) for half in range(2)]
 
     def start_far(point):
-        for t, chosen in enumerate((FAR_LOW, FAR_HIGH)):
+        for half, chosen in enumerate((FAR_LOW, FAR_HIGH)):
             if chosen == point:
-                start(far_copies[3 * t : 3 * t + 3] + far_copies[6 + 3 * t : 9 + 3 * t])
+                start(far_copies[half])
 
     along_z, along_y = (gram_z, iz, n_z, on_z), (gram_y, iy, n_y, on_y)
     second, third = (along_y, along_z) if Y_FIRST else (along_z, along_y)
@@ -444,10 +446,15 @@
 
     if FACTOR_AT == 2:
         blocks = factor_start()
-    wait(far_copies)
-    loop(0, 2, lambda i: primitive_layer(state, prim, 11 * i))
-    loop(0, 2, lambda i: first_layer(state, prim, state2, prim2, 1 + 9 * i))
-    loop(0, 2, lambda i: second_layer(state, state2, prim2, updated, sums, 2 + 7 * i))
+    for half in range(2):
+        wait(far_copies[half])
+        begin, end = CHUNK * half, CHUNK * half + CHUNK
+        for i in range(2):
+            primitive_layer(state, prim, 11 * i, begin, end)
+        for i in range(2):
+            first_layer(state, prim, state2, prim2, 1 + 9 * i, begin, end)
+        for i in range(2):
+            second_layer(state, state2, prim2, updated, sums, 2 + 7 * i, begin, end)
 
     flat_sums = flat(sums)
     columns = []
@@ -471,13 +478,10 @@
             at = (2 * c + half) * 8
             coarse[pl.ds(16 * c + half, 8, stride=2), :] = means[at : at + 8]
 
-    def dot_step(i, acc):
-        for part in range(4):
-            b = 4 * i + part
-            acc = acc + flat_snap[pl.ds(b, 64, stride=BLOCKS), :] * coarse[pl.ds(b, 1), :]
-        return acc
-
-    acc = lax.fori_loop(0, BLOCKS // 4, dot_step, jnp.zeros((64, 128), f32))
+    partial = [jnp.zeros((64, 128), f32) for _ in range(2)]
+    for b in range(BLOCKS):
+        partial[b % 2] = partial[b % 2] + flat_snap[pl.ds(b, 64, stride=BLOCKS), :] * coarse[pl.ds(b, 1), :]
+    acc = partial[0] + partial[1]
     squares = jnp.sum(coarse[...] * coarse[...], axis=0, keepdims=True)
     acc = jnp.where(lax.broadcasted_iota(jnp.int32, (64, 128), 0) == SNAPS, squares, acc)
     ones = jnp.ones((8, 128), bf16)
@@ -529,20 +533,18 @@
 
     lax.fori_loop(0, 1, modes_step, 0)
     store_modes = pltpu.make_async_copy(
-        flat_modes.at[pl.ds(0, SNAPS * BLOCKS)], out_modes.at[pl.ds(0, SNAPS * BLOCKS)], store_sem.at[6]
+        flat_modes.at[pl.ds(0, SNAPS * BLOCKS)], out_modes, store_sem.at[6]
     )
     store_modes.start()
     wait(copies)
     share = total(dot_y, n_y) / rows_all
 
     own = jnp.where(lane < SNAPS, share, 0.0)
-    left = jnp.sum(jnp.where(lane == SNAPS, share, 0.0), axis=1, keepdims=True)[0:1]
-    weights = []
-    for b in range(8):
-        weights.append(jnp.sum(lower_v[b] * own, axis=1, keepdims=True))
-        left = left - jnp.sum(weights[b] * weights[b], axis=0, keepdims=True)
-    last = jnp.broadcast_to(jnp.sqrt(left), (8, 128))
-    mode = [coarse[8 * i : 8 * i + 8, :] for i in range(6)]
+    weights = [jnp.sum(lower_v[b] * own, axis=1, keepdims=True) for b in range(8)]
+    norm = jnp.sum(jnp.where(lane == SNAPS, share, 0.0), axis=1, keepdims=True)[0:1]
+    norm = norm - jnp.sum(sum(weight * weight for weight in weights), axis=0, keepdims=True)
+    last = jnp.broadcast_to(jnp.sqrt(norm), (8, 128))
+    mode = [[coarse[8 * i : 8 * i + 8, :], jnp.zeros((8, 128), f32)] for i in range(6)]
     for b in range(8):
         row = sub + 8 * b
         weight = jnp.broadcast_to(weights[b], (8, 128))
@@ -552,38 +554,27 @@
             one = jnp.broadcast_to(weight[at : at + 1], (8, 128))
             begin = BLOCKS * (8 * b + at)
             for i in range(6):
-                mode[i] = mode[i] - one * flat_modes[begin + 8 * i : begin + 8 * i + 8, :]
+                mode[i][at % 2] = mode[i][at % 2] - one * flat_modes[begin + 8 * i : begin + 8 * i + 8, :]
     scale = 1.0 / last
     for i in range(6):
-        flat_modes[BLOCKS * SNAPS + 8 * i : BLOCKS * SNAPS + 8 * i + 8, :] = mode[i] * scale
-    store_last = pltpu.make_async_copy(
-        flat_modes.at[pl.ds(SNAPS * BLOCKS, BLOCKS)], out_modes.at[pl.ds(SNAPS * BLOCKS, BLOCKS)], store_sem.at[7]
-    )
-    store_last.start()
-    wait(stores + [store_modes, store_last])
+        out_last[8 * i : 8 * i + 8, :] = (mode[i][0] + mode[i][1]) * scale
+    wait(stores + [store_modes])
 
 
 def copy_out(*refs):
-    sources, targets, sem = refs[:5], refs[5:10], refs[10]
+    sources, targets, sem = refs[:6], refs[6:11], refs[11]
     copies = []
 
     def add(source, target):
         copies.append(pltpu.make_async_copy(source, target, sem.at[len(copies)]))
 
-    for source, target in zip(sources, targets):
-        if source.ndim == 4:
-            for c in range(source.shape[0]):
-                for half in range(2):
-                    part = pl.ds(source.shape[1] // 2 * half, source.shape[1] // 2)
-                    add(source.at[c, part], target.at[c, part])
-        elif source.shape[0] == 64:
-            add(source, target)
-        else:
-            pieces = 2 if source.ndim == 3 else 6
-            size = source.shape[0] // pieces
-            for piece in range(pieces):
-                part = pl.ds(size * piece, size)
-                add(source.at[part], target.at[part])
+    add(sources[4], targets[4].at[pl.ds(0, SNAPS * BLOCKS)])
+    add(sources[0], targets[0])
+    for c in range(3):
+        add(sources[1].at[c], targets[1].at[c])
+    add(sources[2], targets[2])
+    add(sources[5], targets[4].at[pl.ds(SNAPS * BLOCKS, BLOCKS)])
+    add(sources[3], targets[3])
     for copy in copies:
         copy.start()
     for copy in copies:
@@ -605,13 +596,14 @@
             functools.partial(kernel, float(rows_all), (n_gx, n_gy, n_y)),
             name="sections_and_modes",
             in_specs=[pl.BlockSpec(memory_space=pltpu.HBM)] * 4,
-            out_specs=(anywhere, anywhere, anywhere, vmem, anywhere),
+            out_specs=(anywhere, anywhere, anywhere, vmem, anywhere, vmem),
             out_shape=(
                 jax.ShapeDtypeStruct((X, Y, Z), f32),
                 jax.ShapeDtypeStruct((3, X, Y, Z), f32),
                 jax.ShapeDtypeStruct((X, Y, Z), f32),
                 jax.ShapeDtypeStruct((64, 64), f32),
-                jax.ShapeDtypeStruct((64 * BLOCKS, 128), f32),
+                jax.ShapeDtypeStruct((SNAPS * BLOCKS, 128), f32),
+                jax.ShapeDtypeStruct((BLOCKS, 128), f32),
             ),
             scratch_shapes=[
                 pltpu.VMEM((5, XP, 2, YP, 128), f32),
@@ -642,9 +634,9 @@
                 pltpu.VMEM((n_y, 8, 128), f32),
                 pltpu.VMEM((4, 8, 128), f32),
                 dma((7,)),
-                dma((8,)),
-                dma((24,)),
-                dma((24,)),
+                dma((7,)),
+                dma((36,)),
+                dma((36,)),
                 dma((2,)),
                 dma((2,)),
                 dma((4,)),
@@ -661,10 +653,11 @@
         new_density, new_momentum, new_energy, factor, modes = pl.pallas_call(
             copy_out,
             name="copy_out",
-            in_specs=[anywhere] * 5,
+            in_specs=[anywhere] * 6,
             out_specs=[pl.BlockSpec(memory_space=pltpu.HBM)] * 5,
-            out_shape=[jax.ShapeDtypeStruct(value.shape, f32) for value in results],
-            scratch_shapes=[dma((17,))],
+            out_shape=[jax.ShapeDtypeStruct(value.shape, f32) for value in results[:4]]
+            + [jax.ShapeDtypeStruct((64 * BLOCKS, 128), f32)],
+            scratch_shapes=[dma((8,))],
             compiler_params=pltpu.CompilerParams(vmem_limit_bytes=2**20),
         )(*results)
         modes = modes.reshape(64, 3, 8, 2, 128).transpose(0, 1, 3, 2, 4).reshape(64, 3, 2, 1024)

time: 45.8 us -> 44.9 us (0.980)
  Pallas kernels: 45.1 us -> 44.2 us
    pallas_call x1, Pallas kernels: 43 us -> 42.1 us  [on_device(): pl.pallas_call(functools.partial(kernel, float(rows_all), (n_gx, n_gy, n_...]
where the time goes in v4:
time: 44.9 us; the launch traced here: 44.8 us
  Pallas kernels  44.2 us (98%)
  between operations  0.64 us (1%)
    pallas_call x1, Pallas kernels, on_device(): pl.pallas_call(functools.partial(kernel, float(rows_all), (n_gx, n_gy, n_...  42.1 us
    pallas_call x1, Pallas kernels, on_device(): pl.pallas_call(copy_out, name='copy_out', in_specs=[anywhere] * 6, out_sp...  2.07 us

profile of v4, /device:TPU:1, one launch (start us, length us, event | category | flops | bytes accessed | tf_op | source)
XLA Modules:
  0.0 44.8 jit_solution(4043972138248575490)
XLA Ops:
  0.6 42.1 %sections_and_modes.1 = (f32[8,64,256]{2,1,0:T(8,128)S(1)}, f32[3,8,64,256]{3,2,1,0:T(8,128)S(1)}, f32[8,64,256]{2,1,0:T(8,128)S(1)}, f32[64,64]{1,0:T(8,128)S(1...) custom-call(f32[8,64,256]{2,1,0:T(8,128)} %density.1, f32[3,8,64,256]{3,2,1,0:T(8,128)} %momentum.1, ...), custom_call_target="tpu_custom_call" | custom-call | tf_op jit(solution)/shard_map/sections_and_modes/pallas_call | solution.py:595
  42.8 2.1 %copy_out.1 = (f32[8,64,256]{2,1,0:T(8,128)}, f32[3,8,64,256]{3,2,1,0:T(8,128)}, f32[8,64,256]{2,1,0:T(8,128)}, f32[64,64]{1,0:T(8,128)}, f32[3072,128]{1,0:T(8,128)}) custom-call(f32[8,64,256]{2,1,0:T(8,128)S(1)} %get-tuple-element.16.refs_0_, f32[3,8,64,256]{3,2,1,0:T(8,128)S(1)} %get-tuple-element.17.refs_1_, ...), custom_call_target="tpu_custom_call" | custom-call | tf_op jit(solution)/shard_map/copy_out/pallas_call | solution.py:653

commit v5 on v4

--- a/solution.py
+++ b/solution.py
@@ -488,7 +488,7 @@
     products = sum(
         lax.dot_general(ones, part, (((1,), (1,)), ((), ())), preferred_element_type=f32) for part in split3(acc)
     )
-    dot_sums[0] = jnp.concatenate([products, jnp.zeros((8, 64), f32)], axis=1)
+    dot_sums[0] = jnp.concatenate([products, jnp.zeros((8, 64), f32)], axis=1)[0:1]
     copies = exchange(lambda peer: dot_sums.at[0], dot_gy, gy, n_gy, on_gy, dot_send, dot_recv, 0)
     dot_gy[gy] = dot_sums[0]
 
@@ -537,7 +537,7 @@
     )
     store_modes.start()
     wait(copies)
-    share = total(dot_y, n_y) / rows_all
+    share = jnp.broadcast_to(total(dot_y, n_y), (8, 128)) / rows_all
 
     own = jnp.where(lane < SNAPS, share, 0.0)
     weights = [jnp.sum(lower_v[b] * own, axis=1, keepdims=True) for b in range(8)]
@@ -629,10 +629,10 @@
                 pltpu.VMEM((n_y, 8, 128), f32),
                 pltpu.VMEM((8, 8, 128), f32),
                 pltpu.VMEM((3, 8, 128), f32),
-                pltpu.VMEM((n_gy, 8, 128), f32),
-                pltpu.VMEM((n_z, 8, 128), f32),
-                pltpu.VMEM((n_y, 8, 128), f32),
-                pltpu.VMEM((4, 8, 128), f32),
+                pltpu.VMEM((n_gy, 1, 128), f32),
+                pltpu.VMEM((n_z, 1, 128), f32),
+                pltpu.VMEM((n_y, 1, 128), f32),
+                pltpu.VMEM((3, 1, 128), f32),
                 dma((7,)),
                 dma((7,)),
                 dma((36,)),

time: 44.9 us -> 44.6 us (level)
  Pallas kernels: 44.2 us -> 43.6 us
    pallas_call x1, Pallas kernels: 42.1 us -> 41.6 us  [on_device(): pl.pallas_call(functools.partial(kernel, float(rows_all), (n_gx, n_gy, n_...]
where the time goes in v5:
time: 44.6 us; the launch traced here: 44.3 us
  Pallas kernels  43.6 us (98%)
  between operations  0.64 us (1%)
    pallas_call x1, Pallas kernels, on_device(): pl.pallas_call(functools.partial(kernel, float(rows_all), (n_gx, n_gy, n_...  41.6 us
    pallas_call x1, Pallas kernels, on_device(): pl.pallas_call(copy_out, name='copy_out', in_specs=[anywhere] * 6, out_sp...  2.07 us

profile of v5, /device:TPU:1, one launch (start us, length us, event | category | flops | bytes accessed | tf_op | source)
XLA Modules:
  0.0 44.3 jit_solution(10924405469125820355)
XLA Ops:
  0.6 41.6 %sections_and_modes.1 = (f32[8,64,256]{2,1,0:T(8,128)S(1)}, f32[3,8,64,256]{3,2,1,0:T(8,128)S(1)}, f32[8,64,256]{2,1,0:T(8,128)S(1)}, f32[64,64]{1,0:T(8,128)S(1...) custom-call(f32[8,64,256]{2,1,0:T(8,128)} %density.1, f32[3,8,64,256]{3,2,1,0:T(8,128)} %momentum.1, ...), custom_call_target="tpu_custom_call" | custom-call | tf_op jit(solution)/shard_map/sections_and_modes/pallas_call | solution.py:595
  42.2 2.1 %copy_out.1 = (f32[8,64,256]{2,1,0:T(8,128)}, f32[3,8,64,256]{3,2,1,0:T(8,128)}, f32[8,64,256]{2,1,0:T(8,128)}, f32[64,64]{1,0:T(8,128)}, f32[3072,128]{1,0:T(8,128)}) custom-call(f32[8,64,256]{2,1,0:T(8,128)S(1)} %get-tuple-element.16.refs_0_, f32[3,8,64,256]{3,2,1,0:T(8,128)S(1)} %get-tuple-element.17.refs_1_, ...), custom_call_target="tpu_custom_call" | custom-call | tf_op jit(solution)/shard_map/copy_out/pallas_call | solution.py:653

commit v6 on v5

--- a/solution.py
+++ b/solution.py
@@ -313,6 +313,11 @@
     def wait(copies):
         for copy in copies:
             copy.wait()
+
+    def arrive(copies):
+        for copy in copies:
+            copy.wait_recv()
+        return copies
 
     def loop(first, stop, step):
         lax.fori_loop(first, stop, lambda x, _: (step(x), 0)[1], 0)
@@ -503,7 +508,7 @@
     start(stores)
     if FACTOR_AT == 0:
         blocks = factor_start()
-    wait(copies)
+    sent = arrive(copies)
     dot_sums[1] = total(dot_gy, n_gy)
     copies = exchange(lambda peer: dot_sums.at[1], dot_z, iz, n_z, on_z, dot_send, dot_recv, 8)
     dot_z[iz] = dot_sums[1]
@@ -516,7 +521,7 @@
         scaled = blocks[b] * (1.0 / jnp.sqrt(diagonal))
         factor_v[b] = jnp.where((lane >= row) & (lane < SNAPS), scaled, 0.0)
         lower_v[b] = jnp.where((row < SNAPS) & (lane < 64), pltpu.roll(scaled, 64, 1), 0.0)
-    wait(copies)
+    sent += arrive(copies)
     dot_sums[2] = total(dot_z, n_z)
     copies = exchange(lambda peer: dot_sums.at[2], dot_y, iy, n_y, on_y, dot_send, dot_recv, 16)
     dot_y[iy] = dot_sums[2]
@@ -536,7 +541,7 @@
         flat_modes.at[pl.ds(0, SNAPS * BLOCKS)], out_modes, store_sem.at[6]
     )
     store_modes.start()
-    wait(copies)
+    sent += arrive(copies)
     share = jnp.broadcast_to(total(dot_y, n_y), (8, 128)) / rows_all
 
     own = jnp.where(lane < SNAPS, share, 0.0)
@@ -559,6 +564,8 @@
     for i in range(6):
         out_last[8 * i : 8 * i + 8, :] = (mode[i][0] + mode[i][1]) * scale
     wait(stores + [store_modes])
+    for copy in sent:
+        copy.wait_send()
 
 
 def copy_out(*refs):

time: 44.6 us -> 44.6 us (level)
  no operation moved by 1% of the time
where the time goes in v6:
time: 44.6 us; the launch traced here: 44.3 us
  Pallas kernels  43.6 us (98%)
  between operations  0.64 us (1%)
    pallas_call x1, Pallas kernels, on_device(): pl.pallas_call(functools.partial(kernel, float(rows_all), (n_gx, n_gy, n_...  41.6 us
    pallas_call x1, Pallas kernels, on_device(): pl.pallas_call(copy_out, name='copy_out', in_specs=[anywhere] * 6, out_sp...  2.07 us

profile of v6, /device:TPU:1, one launch (start us, length us, event | category | flops | bytes accessed | tf_op | source)
XLA Modules:
  0.0 44.3 jit_solution(16440468015017381302)
XLA Ops:
  0.6 41.6 %sections_and_modes.1 = (f32[8,64,256]{2,1,0:T(8,128)S(1)}, f32[3,8,64,256]{3,2,1,0:T(8,128)S(1)}, f32[8,64,256]{2,1,0:T(8,128)S(1)}, f32[64,64]{1,0:T(8,128)S(1...) custom-call(f32[8,64,256]{2,1,0:T(8,128)} %density.1, f32[3,8,64,256]{3,2,1,0:T(8,128)} %momentum.1, ...), custom_call_target="tpu_custom_call" | custom-call | tf_op jit(solution)/shard_map/sections_and_modes/pallas_call | solution.py:602
  42.2 2.1 %copy_out.1 = (f32[8,64,256]{2,1,0:T(8,128)}, f32[3,8,64,256]{3,2,1,0:T(8,128)}, f32[8,64,256]{2,1,0:T(8,128)}, f32[64,64]{1,0:T(8,128)}, f32[3072,128]{1,0:T(8,128)}) custom-call(f32[8,64,256]{2,1,0:T(8,128)S(1)} %get-tuple-element.16.refs_0_, f32[3,8,64,256]{3,2,1,0:T(8,128)S(1)} %get-tuple-element.17.refs_1_, ...), custom_call_target="tpu_custom_call" | custom-call | tf_op jit(solution)/shard_map/copy_out/pallas_call | solution.py:660
